TPU v7x, 32 devices: a whole 2x2x4 slice. The times are simulated.
32 devices in a mesh: shard: 16 (over z, y, x), tensor: 2 (over core).
Axes of the slice: x: 2, y: 2, z: 4, core: 2. Of those that a mesh axis runs over, the one named last changes fastest.
Arguments:
- tokens: bfloat16 [256, 197, 384], P('shard'), may hold values from -6 to 6
- image_counts: int32 [16], P('shard'), may hold values from 8 to 16, as said below
- input_weight: bfloat16 [3, 384, 384], P(None, 'shard', 'tensor')
- query_value_bias: bfloat16 [2, 2, 192], P(None, 'tensor', 'shard'), may hold values from -3 to 3
- output_weight: bfloat16 [384, 384], P('tensor', 'shard'), may hold values from -1.75 to 1.75
- output_bias: bfloat16 [384], P('shard'), may hold values from -3 to 3
- first_gain: bfloat16 [384], P('shard'), may hold values from 0.5 to 1.5
- first_shift: bfloat16 [384], P('shard'), may hold values from -3 to 3
- second_gain: bfloat16 [384], P('shard'), may hold values from 0.5 to 1.5
- second_shift: bfloat16 [384], P('shard'), may hold values from -3 to 3
- expand_weight: bfloat16 [384, 1536], P('shard', 'tensor'), may hold values from -0.3125 to 0.3125
- expand_bias: bfloat16 [2, 768], P('tensor', 'shard'), may hold values from -3 to 3
- reduce_weight: bfloat16 [1536, 384], P('tensor', 'shard'), may hold values from -0.3125 to 0.3125
- reduce_bias: bfloat16 [384], P('shard'), may hold values from -3 to 3
- cotangent: bfloat16 [256, 197, 384], P('shard'), may hold values from -6 to 6
Outputs:
- mixed: bfloat16 [256, 197, 384], P('shard')
- token_grad: bfloat16 [256, 197, 384], P('shard')
- input_weight_grad: float32 [3, 384, 384], P(None, 'shard', 'tensor')
- query_value_bias_grad: float32 [2, 2, 192], P(None, 'tensor', 'shard')
- output_weight_grad: float32 [384, 384], P('tensor', 'shard')
- output_bias_grad: float32 [384], P('shard')
- first_gain_grad: float32 [384], P('shard')
- first_shift_grad: float32 [384], P('shard')
- second_gain_grad: float32 [384], P('shard')
- second_shift_grad: float32 [384], P('shard')
- expand_weight_grad: float32 [384, 1536], P('shard', 'tensor')
- expand_bias_grad: float32 [2, 768], P('tensor', 'shard')
- reduce_weight_grad: float32 [1536, 384], P('tensor', 'shard')
- reduce_bias_grad: float32 [384], P('shard')
Inputs may be any that keep to these rules, and one draw needn't show every extreme that they name: `image_counts`: every index of shard holds at least half of its 16 slots (at least one) filled; some index fills all, some exactly the least.
All inputs are finite; a program needn't handle non-finite values.
Results may differ from a plain program's by a relative error of at most 0.029.
Values may be sent and summed in bfloat16 or wider, within the bound.
No kernel may reach another device: no remote copies, remote signals or barrier semaphores. Data moves between devices by JAX's collectives and lax.ppermute only.
A program may use at most 128 MiB of HBM per device.

v0:
```python
import functools
import math

import jax
import jax.numpy as jnp
from jax import lax
from jax.experimental import pallas as pl
from jax.experimental.pallas import tpu as pltpu
from jax.sharding import PartitionSpec as P

HEAD = 64
EPSILON = 1e-06
LOW = jnp.bfloat16
WIDE = jnp.float32
SMALL = 128
VMEM_LIMIT = 60 * 1024 * 1024


def nn(a, b):
    return jnp.dot(a, b, preferred_element_type=WIDE)


def nt(a, b):
    return lax.dot_general(a, b, (((1,), (1,)), ((), ())), preferred_element_type=WIDE)


def tn(a, b):
    return lax.dot_general(a, b, (((0,), (0,)), ((), ())), preferred_element_type=WIDE)


def padded(length):
    return -(-length // 16) * 16


def stats(hidden):
    center = hidden - jnp.mean(hidden, -1, keepdims=True)
    inverse = lax.rsqrt(jnp.mean(center * center, -1, keepdims=True) + EPSILON)
    return center * inverse, inverse


def norm_back(grad_out, normal, inverse, gain):
    scaled = grad_out * gain
    return inverse * (
        scaled - jnp.mean(scaled, -1, keepdims=True) - normal * jnp.mean(scaled * normal, -1, keepdims=True)
    )


def selection(width, rows, period, offset, start, size, columns):
    row = lax.broadcasted_iota(jnp.int32, (width, columns), 0).astype(WIDE)
    column = lax.broadcasted_iota(jnp.int32, (width, columns), 1).astype(WIDE)
    shard = jnp.floor((row + 0.5) * (1.0 / rows))
    inner = row - shard * rows - start
    hit = (column == shard * period + offset + inner) & (inner >= 0.0) & (inner < size)
    return hit.astype(WIDE).astype(LOW)


def take(ref, at, count, stride):
    return jnp.concatenate([ref[c, pl.ds(at, count, stride=stride), :] for c in range(ref.shape[0])], axis=1)


def put(ref, at, stride, value):
    for c in range(ref.shape[0]):
        ref[c, pl.ds(at, value.shape[0], stride=stride), :] = value[:, c * SMALL : (c + 1) * SMALL]


def put_all(ref, value):
    for c in range(ref.shape[0]):
        ref[c, 0 : value.shape[0]] = value[:, c * SMALL : (c + 1) * SMALL]


def take_all(ref):
    return jnp.concatenate([ref[c] for c in range(ref.shape[0])], axis=1)


def attention_forward(
    rows, scalars, tokens, first, normed_out, qkv_out, probs_out, attended_out, middle_out, joined_out, hold, bias, wide
):
    width = first.shape[1]
    half = width // 2
    length, images = tokens.shape[:2]
    step = pl.program_id(0)

    @pl.when(step == 0)
    def _():
        hold[...] = jnp.zeros_like(hold)
        put_all(wide, tokens[...].astype(WIDE).reshape(length * images, width))
        spare = middle_out.shape[1] - length * images
        middle_out[:, length * images :] = jnp.zeros((middle_out.shape[0], spare, SMALL), WIDE)
        for i in range(4):
            joined_out[:, i * width : (i + 1) * width] = jnp.concatenate(
                [first[0, :, i * half : (i + 1) * half], first[1, :, i * half : (i + 1) * half]], axis=1
            )
        tiny = [first[i, :, 4 * half : 4 * half + SMALL] for i in range(2)]
        same = selection(width, rows, rows, 0, 0, rows, width)
        sel_q = selection(width, rows, rows // 2, 0, 0, rows // 2, half)
        sel_v = selection(width, rows, rows // 2, 0, rows // 2, rows // 2, half)
        shared = tn(tiny[0], same)
        bias[0:1, :width] = shared[0:1]
        bias[1:2, :width] = shared[1:2]
        bias[2:3, :width] = shared[4:5]
        zero = jnp.zeros((1, width), WIDE)
        b_q = jnp.concatenate([tn(t, sel_q)[6:7] for t in tiny], axis=1)
        b_v = jnp.concatenate([tn(t, sel_v)[6:7] for t in tiny], axis=1)
        bias[3:4] = jnp.concatenate([b_q, zero, b_v], axis=1)

    hold[0:length] = take(wide, step, length, images)
    hidden = hold[...]
    normal, _ = stats(hidden)
    normed = (normal * bias[0:1, :width] + bias[1:2, :width]).astype(LOW)
    normed_out[0] = normed
    projected = nn(normed, joined_out[:, : 3 * width]) + bias[3:4]
    queries = (projected[:, :width] * 0.125).astype(LOW)
    keys = projected[:, width : 2 * width].astype(LOW)
    values = projected[:, 2 * width :].astype(LOW)
    qkv_out[0, :, :width] = queries
    qkv_out[0, :, width : 2 * width] = keys
    qkv_out[0, :, 2 * width :] = values
    total = hidden.shape[0]
    lane = lax.broadcasted_iota(jnp.int32, (total, 2 * HEAD), 1)
    first_head = lane < HEAD
    valid = lax.broadcasted_iota(jnp.int32, (1, total), 1) < length
    for pair in range(width // (2 * HEAD)):
        cut = slice(pair * 2 * HEAD, (pair + 1) * 2 * HEAD)
        q_pair, k_pair, v_pair = queries[:, cut], keys[:, cut], values[:, cut]
        outs = []
        for e in range(2):
            mine = first_head if e == 0 else jnp.logical_not(first_head)
            q_one = jnp.where(mine, q_pair, jnp.zeros_like(q_pair))
            scores = jnp.where(valid, nt(q_one, k_pair), -1e30)
            top = jnp.max(scores, -1, keepdims=True)
            power = jnp.exp(scores - top)
            low = (power * (1.0 / jnp.sum(power, -1, keepdims=True))).astype(LOW)
            probs_out[0, 2 * pair + e] = low
            outs.append(nn(low, v_pair))
        attended_out[0, :, cut] = jnp.where(first_head, outs[0], outs[1]).astype(LOW)
    attended = attended_out[0]
    middle = hidden + nt(attended, joined_out[:, 3 * width :]) + bias[2:3, :width]
    put(middle_out, step, images, middle[:length])


def call_attention_forward(rows, scalars, tokens, first, images):
    length, _, width = tokens.shape
    total = padded(length)
    heads = width // HEAD
    flat = padded(length * images)

    def of_image(shape):
        return pl.BlockSpec((1,) + shape, lambda i, s: (i,) + (0,) * len(shape))

    shapes = [((total, width), LOW), ((total, 3 * width), LOW), ((heads, total, total), LOW), ((total, width), LOW)]
    return pl.pallas_call(
        functools.partial(attention_forward, rows),
        grid_spec=pltpu.PrefetchScalarGridSpec(
            num_scalar_prefetch=1,
            grid=(images,),
            in_specs=[
                pl.BlockSpec((length, images, width), lambda i, s: (0, s[0], 0), pipeline_mode=pl.Buffered(1)),
                pl.BlockSpec(first.shape, lambda i, s: (0, 0, 0), pipeline_mode=pl.Buffered(1)),
            ],
            out_specs=[of_image(s) for s, _ in shapes]
            + [pl.BlockSpec((width // SMALL, flat, SMALL), lambda i, s: (0, 0, 0)), pl.BlockSpec((width, 4 * width), lambda i, s: (0, 0))],
            scratch_shapes=[
                pltpu.VMEM((total, width), WIDE),
                pltpu.VMEM((8, 3 * width), WIDE),
                pltpu.VMEM((width // SMALL, length * images, SMALL), WIDE),
            ],
        ),
        out_shape=[jax.ShapeDtypeStruct((images,) + s, d) for s, d in shapes]
        + [jax.ShapeDtypeStruct((width // SMALL, flat, SMALL), WIDE), jax.ShapeDtypeStruct((width, 4 * width), LOW)],
        compiler_params=pltpu.CompilerParams(vmem_limit_bytes=VMEM_LIMIT),
        name="attention_forward",
    )(scalars, tokens, first)


def feed_forward(
    rows, chunk, length, scalars, middle, cotangent, first_small, second, mixed_out, grad_middle_out, own_out, other_out, sums_out,
    bias, own, other,
):
    width = second.shape[1]
    units = second.shape[2] // 2
    step = pl.program_id(0)
    block, images = cotangent.shape[:2]
    count = block * images

    @pl.when(step == 0)
    def _():
        own[...] = jnp.zeros_like(own)
        other[...] = jnp.zeros_like(other)
        sums_out[...] = jnp.zeros_like(sums_out)
        same = selection(width, rows, rows, 0, 0, rows, width)
        shared = tn(first_small[0], same)
        bias[0:1, :width] = shared[2:3]
        bias[1:2, :width] = shared[3:4]
        bias[2:3, :width] = shared[5:6]
        per = units // (width // rows)
        for i in range(2):
            line = jnp.zeros((1, units), WIDE)
            for c in range(per // rows):
                sel = selection(width, rows, per, c * rows, 0, rows, units)
                line = line + tn(first_small[i], sel)[7 + c : 8 + c]
            bias[3 + i : 4 + i, :units] = line

    gain = bias[0:1, :width]
    row = lax.broadcasted_iota(jnp.int32, (count, 1), 0)
    slot = scalars[0] * images + lax.rem(row, images)
    alive = slot < scalars[1]
    held = alive & (step * count + row < length * images)
    top = jnp.where(held, cotangent[...].astype(WIDE).reshape(count, width), 0.0)
    hidden = take_all(middle)
    normal, inverse = stats(hidden)
    normed = (normal * gain + bias[1:2, :width]).astype(LOW)
    top_low = top.astype(LOW)
    normed_t = normed.T
    top_t = top_low.T
    result = hidden + bias[2:3, :width]
    grad_normed = jnp.zeros_like(hidden)
    for i in range(2):
        grads = own if i == 0 else other
        for c in range(units // chunk):
            cut = slice(c * chunk, (c + 1) * chunk)
            cut_low = slice(units + c * chunk, units + (c + 1) * chunk)
            w_expand = second[i, :, cut]
            w_reduce = second[i, :, cut_low]
            before = nn(normed, w_expand) + bias[3 + i : 4 + i, cut]
            share = 0.5 + 0.5 * lax.erf(before * (1.0 / math.sqrt(2.0)))
            slope = share + before * jnp.exp(before * before * -0.5) * (1.0 / math.sqrt(2.0 * math.pi))
            active = (before * share).astype(LOW)
            result = result + nt(active, w_reduce)
            grad_act = nn(top_low, w_reduce).astype(LOW).astype(WIDE)
            grad_before = (grad_act * slope).astype(LOW)
            grad_normed = grad_normed + nt(grad_before, w_expand)
            grads[:, cut] += nn(normed_t, grad_before)
            grads[:, cut_low] += nn(top_t, active)
            sums_out[4 + i : 5 + i, cut] += jnp.sum(grad_before.astype(WIDE), 0, keepdims=True)
    mixed = jnp.where(alive, result, 0.0).reshape(block, images, width)
    mixed_out[...] = mixed.astype(LOW)
    grad_middle = top + norm_back(grad_normed, normal, inverse, gain)
    put_all(grad_middle_out, grad_middle)
    sums_out[0:1, :width] += jnp.sum(grad_normed * normal, 0, keepdims=True)
    sums_out[1:2, :width] += jnp.sum(grad_normed, 0, keepdims=True)
    sums_out[2:3, :width] += jnp.sum(grad_middle, 0, keepdims=True)
    sums_out[3:4, :width] += jnp.sum(top, 0, keepdims=True)

    @pl.when(step == pl.num_programs(0) - 1)
    def _():
        own_out[...] = own[...]
        other_out[...] = other[...].astype(LOW)


def call_feed_forward(rows, scalars, middle, cotangent, first, second, images, steps=3, chunk=256):
    length, _, width = cotangent.shape
    flat = middle.shape[1]
    columns = second.shape[2]
    block = flat // images // steps
    small_at = first.shape[2] // SMALL - 1
    return pl.pallas_call(
        functools.partial(feed_forward, rows, chunk, length),
        grid_spec=pltpu.PrefetchScalarGridSpec(
            num_scalar_prefetch=1,
            grid=(steps,),
            in_specs=[
                pl.BlockSpec((width // SMALL, block * images, SMALL), lambda i, s: (0, i, 0)),
                pl.BlockSpec((block, images, width), lambda i, s: (i, s[0], 0)),
                pl.BlockSpec((2, width, SMALL), lambda i, s: (0, 0, small_at), pipeline_mode=pl.Buffered(1)),
                pl.BlockSpec(second.shape, lambda i, s: (0, 0, 0), pipeline_mode=pl.Buffered(1)),
            ],
            out_specs=[
                pl.BlockSpec((block, images, width), lambda i, s: (i, 0, 0)),
                pl.BlockSpec((width // SMALL, block * images, SMALL), lambda i, s: (0, i, 0)),
                pl.BlockSpec((width, columns), lambda i, s: (0, 0)),
                pl.BlockSpec((width, columns), lambda i, s: (0, 0)),
                pl.BlockSpec((8, columns // 2), lambda i, s: (0, 0)),
            ],
            scratch_shapes=[
                pltpu.VMEM((8, columns // 2), WIDE),
                pltpu.VMEM((width, columns), WIDE),
                pltpu.VMEM((width, columns), WIDE),
            ],
        ),
        out_shape=[
            jax.ShapeDtypeStruct((length, images, width), LOW),
            jax.ShapeDtypeStruct((width // SMALL, flat, SMALL), WIDE),
            jax.ShapeDtypeStruct((width, columns), WIDE),
            jax.ShapeDtypeStruct((width, columns), LOW),
            jax.ShapeDtypeStruct((8, columns // 2), WIDE),
        ],
        compiler_params=pltpu.CompilerParams(vmem_limit_bytes=VMEM_LIMIT),
        name="feed_forward",
    )(scalars, middle, cotangent, first, second)


def attention_backward(
    rows, scalars, tokens, grad_middle, normed, qkv, probs, attended, joined, small, sums_in, token_out, own_out, other_out,
    hold, grads, grad_in, grad_out, sums, gain_row, wide, grads_wide,
):
    length, images, width = tokens.shape
    half = width // 2
    total = normed.shape[1]
    step = pl.program_id(0)

    @pl.when(step == 0)
    def _():
        hold[...] = jnp.zeros_like(hold)
        put_all(wide, tokens[...].astype(WIDE).reshape(length * images, width))
        grad_in[...] = jnp.zeros_like(grad_in)
        grad_out[...] = jnp.zeros_like(grad_out)
        sums[...] = jnp.zeros_like(sums)
        same = selection(width, rows, rows, 0, 0, rows, width)
        gain_row[0:1] = tn(small[0], same)[0:1]

    hold[0:length] = take(grad_middle, step, length, images)
    mid = hold[...]
    mid_low = mid.astype(LOW)
    grad_att = nn(mid_low, joined[:, 3 * width :]).astype(LOW)
    grad_out[...] += tn(mid_low, attended[0])
    lane = lax.broadcasted_iota(jnp.int32, (total, 2 * HEAD), 1)
    first_head = lane < HEAD
    for pair in range(width // (2 * HEAD)):
        cut = slice(pair * 2 * HEAD, (pair + 1) * 2 * HEAD)
        q_pair = qkv[0, :, cut]
        k_pair = qkv[0, :, width + pair * 2 * HEAD : width + (pair + 1) * 2 * HEAD]
        v_pair = qkv[0, :, 2 * width + pair * 2 * HEAD : 2 * width + (pair + 1) * 2 * HEAD]
        g_pair = grad_att[:, cut]
        g_values = g_queries = g_keys = None
        for e in range(2):
            mine = first_head if e == 0 else jnp.logical_not(first_head)
            zero = jnp.zeros_like(q_pair)
            low = probs[0, 2 * pair + e]
            g_one = jnp.where(mine, g_pair, zero)
            weight = low.astype(WIDE)
            slope = nt(g_one, v_pair)
            product = slope * weight
            g_scores = (product - weight * jnp.sum(product, -1, keepdims=True)).astype(LOW)
            parts = (
                tn(low, g_one),
                nn(g_scores, jnp.where(mine, k_pair, zero)),
                tn(g_scores, jnp.where(mine, q_pair, zero)),
            )
            g_values, g_queries, g_keys = (
                parts if e == 0 else (g_values + parts[0], g_queries + parts[1], g_keys + parts[2])
            )
        grads[:, cut] = g_queries.astype(LOW) * jnp.asarray(0.125, LOW)
        grads[:, width + pair * 2 * HEAD : width + (pair + 1) * 2 * HEAD] = g_keys.astype(LOW)
        grads[:, 2 * width + pair * 2 * HEAD : 2 * width + (pair + 1) * 2 * HEAD] = g_values.astype(LOW)
    grad_qkv = grads[...]
    grad_in[...] += tn(normed[0], grad_qkv)
    grad_normed = nt(grad_qkv, joined[:, : 3 * width])
    hold[0:length] = take(wide, step, length, images)
    normal, inverse = stats(hold[...])
    token_grad = mid + norm_back(grad_normed, normal, inverse, gain_row[0:1])
    put(grads_wide, step, images, token_grad[:length])
    sums[0:1, :width] += jnp.sum(grad_normed * normal, 0, keepdims=True)
    sums[1:2, :width] += jnp.sum(grad_normed, 0, keepdims=True)
    sums[2:3] += jnp.sum(grad_qkv.astype(WIDE), 0, keepdims=True)

    @pl.when(step == pl.num_programs(0) - 1)
    def _():
        token_out[...] = take_all(grads_wide).reshape(length, images, width).astype(LOW)
        units = sums_in.shape[1]
        same = selection(width, rows, rows, 0, 0, rows, width)
        sel_q = selection(width, rows, rows // 2, 0, 0, rows // 2, half)
        sel_v = selection(width, rows, rows // 2, 0, rows // 2, rows // 2, half)
        per = units // (width // rows)
        zero = jnp.zeros((1, width), WIDE)

        def lines(block, at, value):
            row = lax.broadcasted_iota(jnp.int32, (SMALL, value.shape[1]), 0)
            new = jnp.where(row == at, value, 0.0)
            return new if block is None else block + new

        shared = None
        for at, value in (
            (0, sums[0:1, :width]), (1, sums[1:2, :width]), (2, sums_in[0:1, :width]), (3, sums_in[1:2, :width]),
            (4, sums_in[2:3, :width]), (5, sums_in[3:4, :width]),
        ):
            shared = lines(shared, at, value)
        common = nt(same, shared.astype(LOW))
        for i in range(2):
            target = own_out if i == 0 else other_out
            for part in range(3):
                at = part * width + i * half
                target[:, part * half : (part + 1) * half] = grad_in[:, at : at + half].astype(target.dtype)
            target[:, 3 * half : 4 * half] = grad_out[:, i * half : (i + 1) * half].astype(target.dtype)
            tiny = common
            tiny = tiny + nt(sel_q, lines(None, 6, sums[2:3, i * half : (i + 1) * half]).astype(LOW))
            tiny = tiny + nt(sel_v, lines(None, 6, sums[2:3, 2 * width + i * half : 2 * width + (i + 1) * half]).astype(LOW))
            for c in range(per // rows):
                sel = selection(width, rows, per, c * rows, 0, rows, units)
                tiny = tiny + nt(sel, lines(None, 7 + c, sums_in[4 + i : 5 + i]).astype(LOW))
            target[:, 4 * half :] = tiny.astype(target.dtype)


def call_attention_backward(rows, scalars, tokens, grad_middle, normed, qkv, probs, attended, joined, first, sums_in, images):
    length, _, width = tokens.shape
    total = normed.shape[1]
    columns = first.shape[2]
    small_at = columns // SMALL - 1

    def of_image(array):
        return pl.BlockSpec((1,) + array.shape[1:], lambda i, s: (i,) + (0,) * (array.ndim - 1))

    def whole(array):
        return pl.BlockSpec(array.shape, lambda i, s: (0,) * array.ndim, pipeline_mode=pl.Buffered(1))

    return pl.pallas_call(
        functools.partial(attention_backward, rows),
        grid_spec=pltpu.PrefetchScalarGridSpec(
            num_scalar_prefetch=1,
            grid=(images,),
            in_specs=[
                pl.BlockSpec((length, images, width), lambda i, s: (0, s[0], 0), pipeline_mode=pl.Buffered(1)),
                whole(grad_middle), of_image(normed), of_image(qkv), of_image(probs), of_image(attended),
                whole(joined),
                pl.BlockSpec((2, width, SMALL), lambda i, s: (0, 0, small_at), pipeline_mode=pl.Buffered(1)),
                whole(sums_in),
            ],
            out_specs=[
                pl.BlockSpec((length, images, width), lambda i, s: (0, 0, 0)),
                pl.BlockSpec((width, columns), lambda i, s: (0, 0)),
                pl.BlockSpec((width, columns), lambda i, s: (0, 0)),
            ],
            scratch_shapes=[
                pltpu.VMEM((total, width), WIDE),
                pltpu.VMEM((total, 3 * width), LOW),
                pltpu.VMEM((width, 3 * width), WIDE),
                pltpu.VMEM((width, width), WIDE),
                pltpu.VMEM((8, 3 * width), WIDE),
                pltpu.VMEM((8, width), WIDE),
                pltpu.VMEM((width // SMALL, length * images, SMALL), WIDE),
                pltpu.VMEM((width // SMALL, length * images, SMALL), WIDE),
            ],
        ),
        out_shape=[
            jax.ShapeDtypeStruct((length, images, width), LOW),
            jax.ShapeDtypeStruct((width, columns), WIDE),
            jax.ShapeDtypeStruct((width, columns), LOW),
        ],
        compiler_params=pltpu.CompilerParams(vmem_limit_bytes=VMEM_LIMIT),
        name="attention_backward",
    )(scalars, tokens, grad_middle, normed, qkv, probs, attended, joined, first, sums_in)


def stages_of(count):
    found = []
    stride = 1
    while stride < count:
        radix = 4 if (count // stride) % 4 == 0 else 2
        found.append((stride, radix))
        stride *= radix
    return found[::-1]


def hop(array, count, offset):
    return lax.ppermute(array, "shard", [(i, i ^ offset) for i in range(count)])


def swap(array):
    return lax.ppermute(array, "tensor", [(0, 1), (1, 0)])


def gather_pieces(piece, count):
    held, owners = piece[None], [0]
    levels = stages_of(count)
    for at, (stride, radix) in enumerate(levels):
        got = [held] + [hop(held, count, k * stride) for k in range(1, radix)]
        marks = [[o ^ (k * stride) for o in owners] for k in range(radix)]
        if at + 1 < len(levels):
            held, owners = jnp.concatenate(got), sum(marks, [])
    return got, marks


def assemble(scalars, got, marks, count):
    arrays = got + [swap(g) for g in got]
    places = [(half, a, b, mark) for half in range(2) for a, line in enumerate(marks) for b, mark in enumerate(line)]

    def kernel(scalars, *refs):
        ins, out, sems = refs[: len(arrays)], refs[-2], refs[-1]
        copies = []
        for at, (half, a, b, mark) in enumerate(places):
            owner = lax.bitwise_xor(scalars[2], mark)
            source = ins[half * len(got) + a].at[b]
            copies.append(pltpu.make_async_copy(source, out.at[half, owner], sems.at[at]))
        for copy in copies:
            copy.start()
        for copy in copies:
            copy.wait()

    shape = (2, count) + got[0].shape[1:]
    anywhere = pl.BlockSpec(memory_space=pl.ANY)
    return pl.pallas_call(
        kernel,
        in_specs=[pl.BlockSpec(memory_space=pltpu.SMEM)] + [anywhere] * len(arrays),
        out_specs=anywhere,
        scratch_shapes=[pltpu.SemaphoreType.DMA((len(places),))],
        out_shape=jax.ShapeDtypeStruct(shape, LOW),
        name="assemble",
    )(scalars, *arrays)


def combine(scalars, arrays, stride, radix):
    blocks, rows, columns = arrays[0].shape
    high = blocks // radix

    def kernel(scalars, *refs):
        outs = refs[len(arrays) * radix :]
        for k in range(radix):
            total = None
            for a in range(len(arrays)):
                value = refs[a * radix + k][0].astype(WIDE)
                total = value if total is None else total + value
            outs[k][0] = total.astype(outs[k].dtype)

    def block(k):
        def index(i, s):
            return (i * radix + (lax.rem(lax.div(s[2], stride), radix) ^ k), 0, 0)

        return pl.BlockSpec((1, rows, columns), index)

    return pl.pallas_call(
        kernel,
        grid_spec=pltpu.PrefetchScalarGridSpec(
            num_scalar_prefetch=1,
            grid=(high,),
            in_specs=[block(k) for _ in arrays for k in range(radix)],
            out_specs=[pl.BlockSpec((1, rows, columns), lambda i, s: (i, 0, 0))] * radix,
        ),
        out_shape=[jax.ShapeDtypeStruct((high, rows, columns), LOW if k else WIDE) for k in range(radix)],
        name="combine",
    )(scalars, *[a for a in arrays for _ in range(radix)])


def scatter_rows(scalars, own, received, count):
    arrays = [own, received]
    for stride, radix in stages_of(count)[::-1]:
        sums = combine(scalars, arrays, stride, radix)
        arrays = [sums[0]] + [hop(sums[k], count, k * stride) for k in range(1, radix)]
    return arrays


def total_of(refs):
    total = refs[0][0]
    for ref in refs[1:]:
        total = total + ref[0].astype(WIDE)
    return total


def finish_second(arrays, units):
    rows = arrays[0].shape[1]

    def kernel(*refs):
        total = total_of(refs[:-2])
        refs[-2][...] = total[:, :units]
        refs[-1][...] = total[:, units:]

    return pl.pallas_call(
        kernel, out_shape=[jax.ShapeDtypeStruct((rows, units), WIDE)] * 2, name="finish_second"
    )(*arrays)


def finish_first(arrays, half, units):
    rows = arrays[0].shape[1]
    per = units // (2 * half // rows)

    def kernel(*refs):
        outs = refs[len(arrays) :]
        total = total_of(refs[: len(arrays)])
        for i in range(3):
            outs[0][i] = total[:, i * half : (i + 1) * half]
        outs[1][...] = total[:, 3 * half : 4 * half]
        tiny = total[:, 4 * half :]

        def line(at, start, size, columns, shift):
            row = lax.broadcasted_iota(jnp.int32, (rows, columns), 0) - start
            lane = lax.broadcasted_iota(jnp.int32, (rows, columns), 1) - shift
            hit = (row == lane) & (row >= 0) & (row < size)
            return jnp.sum(jnp.where(hit, tiny[:, at : at + 1], 0.0), 0, keepdims=True)

        for i in range(6):
            outs[2 + i][...] = line(i, 0, rows, rows, 0)
        for i in range(2):
            outs[8][i] = line(6, i * (rows // 2), rows // 2, rows // 2, 0)
        wide = line(7, 0, rows, per, 0)
        for c in range(1, per // rows):
            wide = wide + line(7 + c, 0, rows, per, c * rows)
        outs[9][...] = wide

    shapes = [(3, rows, half), (rows, half)] + [(1, rows)] * 6 + [(2, 1, rows // 2), (1, per)]
    return pl.pallas_call(
        kernel, out_shape=[jax.ShapeDtypeStruct(s, WIDE) for s in shapes], name="finish_first"
    )(*arrays)


def join(scalars, array):
    length, images, width = array.shape
    other = swap(array)

    def kernel(scalars, own, other, out, sems):
        here = pltpu.make_async_copy(own, out.at[:, scalars[0]], sems.at[0])
        there = pltpu.make_async_copy(other, out.at[:, 1 - scalars[0]], sems.at[1])
        here.start()
        there.start()
        here.wait()
        there.wait()

    anywhere = pl.BlockSpec(memory_space=pl.ANY)
    out = pl.pallas_call(
        kernel,
        in_specs=[pl.BlockSpec(memory_space=pltpu.SMEM), anywhere, anywhere],
        out_specs=anywhere,
        scratch_shapes=[pltpu.SemaphoreType.DMA((2,))],
        out_shape=jax.ShapeDtypeStruct((length, 2, images, width), array.dtype),
        name="join",
    )(scalars, array, other)
    return out.reshape(length, 2 * images, width).transpose(1, 0, 2)


def pack_small(columns):
    block = jnp.stack(columns, axis=-1)
    return jnp.pad(block, [(0, 0), (0, SMALL - block.shape[-1])])


def body(shards, tokens, image_counts, input_weight, query_value_bias, output_weight, output_bias, first_gain,
         first_shift, second_gain, second_shift, expand_weight, expand_bias, reduce_weight, reduce_bias, cotangent):
    rows, half = input_weight.shape[1:]
    units = expand_weight.shape[1]
    width = rows * shards
    images = tokens.shape[0] // 2
    scalars = jnp.stack([lax.axis_index("tensor"), image_counts[0], lax.axis_index("shard")]).astype(jnp.int32)
    small = pack_small(
        [first_gain, first_shift, second_gain, second_shift, output_bias, reduce_bias, query_value_bias.reshape(-1)]
        + list(expand_bias.reshape(-1, rows)))
    first = jnp.concatenate([input_weight[0], input_weight[1], input_weight[2], output_weight.T, small], axis=1)
    second = jnp.concatenate([expand_weight, reduce_weight.T], axis=1)
    first = assemble(scalars, *gather_pieces(first, shards), shards).reshape(2, width, -1)
    second = assemble(scalars, *gather_pieces(second, shards), shards).reshape(2, width, -1)
    tokens = tokens.transpose(1, 0, 2)
    cotangent = cotangent.transpose(1, 0, 2)
    normed, qkv, probs, attended, middle, joined = call_attention_forward(rows, scalars, tokens, first, images)
    mixed, grad_middle, own, other, sums = call_feed_forward(rows, scalars, middle, cotangent, first, second, images)

    def spread(own, other):
        shape = (shards, rows, -1)
        return scatter_rows(scalars, own.reshape(shape), swap(other).reshape(shape), shards)

    grad_expand, grad_reduce = finish_second(spread(own, other), units)
    token_grad, own, other = call_attention_backward(
        rows, scalars, tokens, grad_middle, normed, qkv, probs, attended, joined, first, sums, images)
    outs = finish_first(spread(own, other), half, units)
    gains = [o.reshape(rows) for o in outs[2:8]]
    return (
        join(scalars, mixed),
        join(scalars, token_grad),
        outs[0],
        outs[8],
        outs[1].T,
        gains[4],
        gains[0],
        gains[1],
        gains[2],
        gains[3],
        grad_expand,
        outs[9],
        grad_reduce.T,
        gains[5],
    )


def solution(mesh):
    in_specs = (
        P("shard", None, None),
        P("shard"),
        P(None, "shard", "tensor"),
        P(None, "tensor", "shard"),
        P("tensor", "shard"),
        P("shard"),
        P("shard"),
        P("shard"),
        P("shard"),
        P("shard"),
        P("shard", "tensor"),
        P("tensor", "shard"),
        P("tensor", "shard"),
        P("shard"),
        P("shard", None, None),
    )
    out_specs = in_specs[:1] + in_specs[-1:] + in_specs[2:-1]
    assert mesh.shape["tensor"] == 2
    return jax.shard_map(
        functools.partial(body, mesh.shape["shard"]), mesh=mesh, in_specs=in_specs, out_specs=out_specs, check_vma=False
    )
```

profile of v0, /device:TPU:0, one launch (start us, length us, event | category | flops | bytes accessed | tf_op | source)
XLA Modules:
  0.0 439.5 jit_solution(6048147786755634342)
XLA Ops:
  0.6 0.8 slice_bitcast_fusion.3
  1.6 0.7 stack_reshape.4
  2.4 0.8 copy.33
  3.1 0.7 copy.29
  3.9 0.7 copy.30
  4.6 0.7 copy.31
  5.4 0.7 copy.32
  6.1 0.7 copy.34
  6.9 0.7 slice_bitcast_fusion
  7.7 0.8 concatenate.12
  8.5 5.1 %collective-permute-start.2 = (bf16[1,24,896]{2,1,0:T(8,128)(2,1)S(1)}, bf16[1,24,896]{2,1,0:T(8,128)(2,1)S(1)}, u32[]{:S(2)}, u32[]{:S(2)}) collective-permute-start(bf16[1,24,896]{2,1,0:T(8,128)(2,1)S(1)} %bitcast.72), channel_id=1, source_target_pairs={{0,24},{2,26},{4,28},{6,30},{8,16},{10,18},{12,20},{14,22},{16,8},... | collective-permute-start | bytes 129032 | tf_op jit(solution)/shard_map/ppermute | solution.py:454
  14.3 0.8 maximum_bitcast_fusion
  15.1 3.7 collective-permute-start.12
  20.0 2.5 collective-permute-start.5
  22.5 0.8 collective-permute-start.4
  23.3 1.3 collective-permute-done.11
  24.7 2.5 collective-permute-start.15
  28.3 1.5 collective-permute-start.3
  29.8 8.0 %collective-permute-done.4.refs_2_ = bf16[4,24,896]{2,1,0:T(8,128)(2,1)S(1)} collective-permute-done((bf16[4,24,896]{2,1,0:T(8,128)(2,1)S(1)}, bf16[4,24,896]{2,1,0:T(8,128)(2,1)S(1)}, u32[]{:S(2)}, u32[]{:S(2)}) %collective-permute-start.4) | collective-permute-done | bytes 172064 | tf_op jit(solution)/shard_map/ppermute | solution.py:454
  37.7 6.4 %collective-permute-done.3.refs_1_ = bf16[4,24,896]{2,1,0:T(8,128)(2,1)S(1)} collective-permute-done((bf16[4,24,896]{2,1,0:T(8,128)(2,1)S(1)}, bf16[4,24,896]{2,1,0:T(8,128)(2,1)S(1)}, u32[]{:S(2)}, u32[]{:S(2)}) %collective-permute-start.3) | collective-permute-done | bytes 172064 | tf_op jit(solution)/shard_map/ppermute | solution.py:454
  47.8 43.8 %assemble.2 = bf16[2,16,24,896]{3,2,1,0:T(8,128)(2,1)} custom-call(s32[3]{0:T(128)} %pad_add_fusion.scalars, bf16[4,24,896]{2,1,0:T(8,128)(2,1)} %copy-done.10, bf16[4,24,896]{2,1,0:T(8,128)(2,1)} %copy-done.21, bf16[4,24,896]{2,1,0:T(8,128)(2,1)} %copy-done.20, bf16[4,24,896]{2,1,0:T(8,128)(2,1)} %copy-done.19, bf16[4,24,896]{2,1,0:T(8,128)(2,1)} %copy-done.18, ...), custom_call_target="tpu_custom_call" | custom-call | tf_op jit(solution)/shard_map/assemble/pallas_call | solution.py:490
  91.6 18.5 %attention_forward.1 = (bf16[8,208,384]{2,1,0:T(8,128)(2,1)}, bf16[8,208,1152]{2,1,0:T(8,128)(2,1)}, bf16[8,6,208,208]{3,2,1,0:T(8,128)(2,1)}, bf16[8,208,384]{2...) custom-call(s32[3]{0:T(128)} %pad_add_fusion.scalars, bf16[197,16,384]{2,1,0:T(8,128)(2,1)} %bitcast.66, ...), custom_call_target="tpu_custom_call" | custom-call | tf_op jit(solution)/shard_map/attention_forward/pallas_call | solution.py:151
  111.8 73.5 %assemble.3 = bf16[2,16,24,1536]{3,2,1,0:T(8,128)(2,1)} custom-call(s32[3]{0:T(128)} %pad_add_fusion.scalars, bf16[4,24,1536]{2,1,0:T(8,128)(2,1)} %copy-done.9, bf16[4,24,1536]{2,1,0:T(8,128)(2,1)} %copy-done.13, bf16[4,24,1536]{2,1,0:T(8,128)(2,1)} %copy-done.12, bf16[4,24,1536]{2,1,0:T(8,128)(2,1)} %copy-done.11, bf16[4,24,1536]{2,1,0:T(8,128)(2,1)} %copy-done.14, ...), custom_call_target="tpu_custom_call" | custom-call | tf_op jit(solution)/shard_map/assemble/pallas_call | solution.py:490
  185.4 26.9 %feed_forward.1 = (bf16[197,8,384]{2,1,0:T(8,128)(2,1)}, f32[3,1584,128]{2,1,0:T(8,128)}, f32[384,1536]{1,0:T(8,128)}, bf16[384,1536]{1,0:T(8,128)(2,1)}, f32[8,768]{1,0:T(8,128)}) custom-call(s32[3]{0:T(128)} %pad_add_fusion.scalars, f32[3,1584,128]{2,1,0:T(8,128)} %get-tuple-element.56.middle, bf16[197,16,384]{2,1,0:T(8,128)(2,1)} %bitcast.71, ...), custom_call_target="tpu_custom_call" | custom-call | tf_op jit(solution)/shard_map/feed_forward/pallas_call | solution.py:256
  212.6 29.3 %attention_backward.1 = (bf16[197,8,384]{2,1,0:T(8,128)(2,1)}, f32[384,896]{1,0:T(8,128)}, bf16[384,896]{1,0:T(8,128)(2,1)}) custom-call(s32[3]{0:T(128)} %pad_add_fusion.scalars, bf16[197,16,384]{2,1,0:T(8,128)(2,1)} %bitcast.67, f32[3,1584,128]{2,1,0:T(8,128)} %get-tuple-element.58.grad_middle, bf16[8,208,384]{2,1,0:T(8,128)(2,1)} %get-tuple-element.59.normed, ...), custom_call_target="tpu_custom_call" | custom-call | tf_op jit(solution)/shard_map/attention_backward/pallas_call | solution.py:405
  242.6 1.6 collective-permute-done.22
  244.2 0.9 copy-done.1
  245.1 4.3 combine.4
  249.3 1.5 collective-permute-start.23
  251.4 1.5 collective-permute-start.25
  252.9 4.8 %combine.6 = (f32[4,24,1536]{2,1,0:T(8,128)}, bf16[4,24,1536]{2,1,0:T(8,128)(2,1)}, bf16[4,24,1536]{2,1,0:T(8,128)(2,1)}, bf16[4,24,1536]{2,1,0:T(8,128)(2,1)}) custom-call(s32[3]{0:T(128)} %pad_add_fusion.scalars, f32[16,24,1536]{2,1,0:T(8,128)} %bitcast.47, f32[16,24,1536]{2,1,0:T(8,128)} %bitcast.48, f32[16,24,1536]{2,1,0:T(8,128)} %bitcast.49, ...), custom_call_target="tpu_custom_call" | custom-call | tf_op jit(solution)/shard_map/combine/pallas_call | solution.py:519
  257.7 1.6 collective-permute-start.30
  259.2 1.8 collective-permute-done.24.refs_8_.refs_9_.refs_10_.refs_11_
  261.6 1.5 collective-permute-start.32
  263.1 2.5 combine.5
  265.6 2.3 collective-permute-done.30.refs_4_.refs_5_.refs_6_.refs_7_
  267.9 1.0 collective-permute-start.26
  268.9 5.4 %collective-permute-done.31.refs_8_.refs_9_.refs_10_.refs_11_ = bf16[4,24,1536]{2,1,0:T(8,128)(2,1)S(1)} collective-permute-done((bf16[4,24,1536]{2,1,0:T(8,128)(2,1)}, bf16[4,24,1536]{2,1,0:T(8,128)(2,1)S(1)}, u32[]{:S(2)}, u32[]{:S(2)}) %collective-permute-start.31) | collective-permute-done | bytes 294944 | tf_op jit(solution)/shard_map/ppermute | solution.py:454
  274.3 1.9 collective-permute-start.27
  276.2 1.5 collective-permute-start.28
  277.8 2.9 combine.7
  280.7 1.2 collective-permute-start.33
  281.9 1.7 collective-permute-start.34
  283.6 1.5 collective-permute-start.35
  285.1 1.6 finish_first.1
  286.8 75.1 %join.3 = bf16[197,2,8,384]{3,2,1,0:T(8,128)(2,1)} custom-call(s32[3]{0:T(128)} %pad_add_fusion.scalars, bf16[197,8,384]{2,1,0:T(8,128)(2,1)} %get-tuple-element.65.own, bf16[197,8,384]{2,1,0:T(8,128)(2,1)} %collective-permute-done.21.other), custom_call_target="tpu_custom_call" | custom-call | tf_op jit(solution)/shard_map/join/pallas_call | solution.py:606
  361.9 75.1 %join.2 = bf16[197,2,8,384]{3,2,1,0:T(8,128)(2,1)} custom-call(s32[3]{0:T(128)} %pad_add_fusion.scalars, bf16[197,8,384]{2,1,0:T(8,128)(2,1)} %get-tuple-element.57.own, bf16[197,8,384]{2,1,0:T(8,128)(2,1)} %collective-permute-done.20.other), custom_call_target="tpu_custom_call" | custom-call | tf_op jit(solution)/shard_map/join/pallas_call | solution.py:606
  437.8 1.7 finish_second.1
  (115 shorter events, 10.7 us)
Async XLA Ops:
  8.5 10.3 %collective-permute-start.2 = (bf16[1,24,896]{2,1,0:T(8,128)(2,1)S(1)}, bf16[1,24,896]{2,1,0:T(8,128)(2,1)S(1)}, u32[]{:S(2)}, u32[]{:S(2)}) collective-permute-start(bf16[1,24,896]{2,1,0:T(8,128)(2,1)S(1)} %bitcast.72), channel_id=1, source_target_pairs={{0,24},{2,26},{4,28},{6,30},{8,16},{10,18},{12,20},{14,22},{16,8},... | collective-permute-start | bytes 129032 | tf_op jit(solution)/shard_map/ppermute | solution.py:454
  13.7 6.2 %collective-permute-start.1 = (bf16[1,24,896]{2,1,0:T(8,128)(2,1)S(1)}, bf16[1,24,896]{2,1,0:T(8,128)(2,1)S(1)}, u32[]{:S(2)}, u32[]{:S(2)}) collective-permute-start(bf16[1,24,896]{2,1,0:T(8,128)(2,1)S(1)} %bitcast.73), channel_id=1, source_target_pairs={{0,16},{2,18},{4,20},{6,22},{8,24},{10,26},{12,28},{14,30},{16,0},... | collective-permute-start | bytes 129032 | tf_op jit(solution)/shard_map/ppermute | solution.py:454
  13.7 6.2 %collective-permute-start = (bf16[1,24,896]{2,1,0:T(8,128)(2,1)S(1)}, bf16[1,24,896]{2,1,0:T(8,128)(2,1)S(1)}, u32[]{:S(2)}, u32[]{:S(2)}) collective-permute-start(bf16[1,24,896]{2,1,0:T(8,128)(2,1)S(1)} %bitcast.74), channel_id=1, source_target_pairs={{0,8},{2,10},{4,12},{6,14},{8,0},{10,2},{12,4},{14,6},{16,24},{18,... | collective-permute-start | bytes 129032 | tf_op jit(solution)/shard_map/ppermute | solution.py:454
  15.1 7.4 %collective-permute-start.12 = (bf16[1,24,1536]{2,1,0:T(8,128)(2,1)S(1)}, bf16[1,24,1536]{2,1,0:T(8,128)(2,1)S(1)}, u32[]{:S(2)}, u32[]{:S(2)}) collective-permute-start(bf16[1,24,1536]{2,1,0:T(8,128)(2,1)S(1)} %maximum_bitcast_fusion), channel_id=1, source_target_pairs={{0,24},{2,26},{4,28},{6,30},{8,16},{10,18},{12,20},{14,22},{16,8},... | collective-permute-start | bytes 221192 | tf_op jit(solution)/shard_map/ppermute | solution.py:454
  18.9 5.7 %collective-permute-start.11 = (bf16[1,24,1536]{2,1,0:T(8,128)(2,1)S(1)}, bf16[1,24,1536]{2,1,0:T(8,128)(2,1)S(1)}, u32[]{:S(2)}, u32[]{:S(2)}) collective-permute-start(bf16[1,24,1536]{2,1,0:T(8,128)(2,1)S(1)} %maximum_bitcast_fusion), channel_id=1, source_target_pairs={{0,16},{2,18},{4,20},{6,22},{8,24},{10,26},{12,28},{14,30},{16,0},... | collective-permute-start | bytes 221192 | tf_op jit(solution)/shard_map/ppermute | solution.py:454
  18.9 5.8 %collective-permute-start.10 = (bf16[1,24,1536]{2,1,0:T(8,128)(2,1)S(1)}, bf16[1,24,1536]{2,1,0:T(8,128)(2,1)S(1)}, u32[]{:S(2)}, u32[]{:S(2)}) collective-permute-start(bf16[1,24,1536]{2,1,0:T(8,128)(2,1)S(1)} %maximum_bitcast_fusion), channel_id=1, source_target_pairs={{0,8},{2,10},{4,12},{6,14},{8,0},{10,2},{12,4},{14,6},{16,24},{18,... | collective-permute-start | bytes 221192 | tf_op jit(solution)/shard_map/ppermute | solution.py:454
  19.9 27.9 %copy-start.10 = (bf16[4,24,896]{2,1,0:T(8,128)(2,1)}, bf16[4,24,896]{2,1,0:T(8,128)(2,1)S(1)}, u32[]{:S(2)}) copy-start(bf16[4,24,896]{2,1,0:T(8,128)(2,1)S(1)} %pad_maximum_fusion.1.refs_0_) | copy-start | bytes 516100
  19.9 7.8 %collective-permute-start.6 = (bf16[4,24,896]{2,1,0:T(8,128)(2,1)S(1)}, bf16[4,24,896]{2,1,0:T(8,128)(2,1)S(1)}, u32[]{:S(2)}, u32[]{:S(2)}) collective-permute-start(bf16[4,24,896]{2,1,0:T(8,128)(2,1)S(1)} %pad_maximum_fusion.1.refs_0_), channel_id=1, source_target_pairs={{0,1},{1,0},{2,3},{3,2},{4,5},{5,4},{6,7},{7,6},{8,9},{9,8},{10,11... | collective-permute-start | bytes 516104 | tf_op jit(solution)/shard_map/ppermute | solution.py:458
  20.0 8.3 %collective-permute-start.5 = (bf16[4,24,896]{2,1,0:T(8,128)(2,1)S(1)}, bf16[4,24,896]{2,1,0:T(8,128)(2,1)S(1)}, u32[]{:S(2)}, u32[]{:S(2)}) collective-permute-start(bf16[4,24,896]{2,1,0:T(8,128)(2,1)S(1)} %pad_maximum_fusion.1.refs_0_), channel_id=1, source_target_pairs={{0,6},{2,4},{4,2},{6,0},{8,14},{10,12},{12,10},{14,8},{16,22},{18,... | collective-permute-start | bytes 516104 | tf_op jit(solution)/shard_map/ppermute | solution.py:454
  22.5 15.2 %collective-permute-start.4 = (bf16[4,24,896]{2,1,0:T(8,128)(2,1)S(1)}, bf16[4,24,896]{2,1,0:T(8,128)(2,1)S(1)}, u32[]{:S(2)}, u32[]{:S(2)}) collective-permute-start(bf16[4,24,896]{2,1,0:T(8,128)(2,1)S(1)} %pad_maximum_fusion.1.refs_0_), channel_id=1, source_target_pairs={{0,4},{2,6},{4,0},{6,2},{8,12},{10,14},{12,8},{14,10},{16,20},{18,... | collective-permute-start | bytes 516104 | tf_op jit(solution)/shard_map/ppermute | solution.py:454
  24.7 66.9 %copy-start.9 = (bf16[4,24,1536]{2,1,0:T(8,128)(2,1)}, bf16[4,24,1536]{2,1,0:T(8,128)(2,1)S(1)}, u32[]{:S(2)}) copy-start(bf16[4,24,1536]{2,1,0:T(8,128)(2,1)S(1)} %pad_maximum_fusion.refs_0_) | copy-start | bytes 884740
  24.7 19.4 %collective-permute-start.15 = (bf16[4,24,1536]{2,1,0:T(8,128)(2,1)S(1)}, bf16[4,24,1536]{2,1,0:T(8,128)(2,1)S(1)}, u32[]{:S(2)}, u32[]{:S(2)}) collective-permute-start(bf16[4,24,1536]{2,1,0:T(8,128)(2,1)S(1)} %pad_maximum_fusion.refs_0_), channel_id=1, source_target_pairs={{0,6},{2,4},{4,2},{6,0},{8,14},{10,12},{12,10},{14,8},{16,22},{18,... | collective-permute-start | bytes 884744 | tf_op jit(solution)/shard_map/ppermute | solution.py:454
  27.2 17.4 %collective-permute-start.14 = (bf16[4,24,1536]{2,1,0:T(8,128)(2,1)S(1)}, bf16[4,24,1536]{2,1,0:T(8,128)(2,1)S(1)}, u32[]{:S(2)}, u32[]{:S(2)}) collective-permute-start(bf16[4,24,1536]{2,1,0:T(8,128)(2,1)S(1)} %pad_maximum_fusion.refs_0_), channel_id=1, source_target_pairs={{0,4},{2,6},{4,0},{6,2},{8,12},{10,14},{12,8},{14,10},{16,20},{18,... | collective-permute-start | bytes 884744 | tf_op jit(solution)/shard_map/ppermute | solution.py:454
  27.7 20.0 %copy-start.18 = (bf16[4,24,896]{2,1,0:T(8,128)(2,1)}, bf16[4,24,896]{2,1,0:T(8,128)(2,1)S(1)}, u32[]{:S(2)}) copy-start(bf16[4,24,896]{2,1,0:T(8,128)(2,1)S(1)} %collective-permute-done.6.refs_4_) | copy-start | bytes 516100
  27.7 17.0 %collective-permute-start.13 = (bf16[4,24,1536]{2,1,0:T(8,128)(2,1)S(1)}, bf16[4,24,1536]{2,1,0:T(8,128)(2,1)S(1)}, u32[]{:S(2)}, u32[]{:S(2)}) collective-permute-start(bf16[4,24,1536]{2,1,0:T(8,128)(2,1)S(1)} %pad_maximum_fusion.refs_0_), channel_id=1, source_target_pairs={{0,2},{2,0},{4,6},{6,4},{8,10},{10,8},{12,14},{14,12},{16,18},{18,... | collective-permute-start | bytes 884744 | tf_op jit(solution)/shard_map/ppermute | solution.py:454
  28.3 19.5 %copy-start.19 = (bf16[4,24,896]{2,1,0:T(8,128)(2,1)}, bf16[4,24,896]{2,1,0:T(8,128)(2,1)S(1)}, u32[]{:S(2)}) copy-start(bf16[4,24,896]{2,1,0:T(8,128)(2,1)S(1)} %collective-permute-done.5.refs_3_) | copy-start | bytes 516100
  28.3 15.9 %collective-permute-start.3 = (bf16[4,24,896]{2,1,0:T(8,128)(2,1)S(1)}, bf16[4,24,896]{2,1,0:T(8,128)(2,1)S(1)}, u32[]{:S(2)}, u32[]{:S(2)}) collective-permute-start(bf16[4,24,896]{2,1,0:T(8,128)(2,1)S(1)} %pad_maximum_fusion.1.refs_0_), channel_id=1, source_target_pairs={{0,2},{2,0},{4,6},{6,4},{8,10},{10,8},{12,14},{14,12},{16,18},{18,... | collective-permute-start | bytes 516104 | tf_op jit(solution)/shard_map/ppermute | solution.py:454
  37.7 10.0 %copy-start.20 = (bf16[4,24,896]{2,1,0:T(8,128)(2,1)}, bf16[4,24,896]{2,1,0:T(8,128)(2,1)S(1)}, u32[]{:S(2)}) copy-start(bf16[4,24,896]{2,1,0:T(8,128)(2,1)S(1)} %collective-permute-done.4.refs_2_) | copy-start | bytes 516100
  37.7 7.4 %collective-permute-start.9 = (bf16[4,24,896]{2,1,0:T(8,128)(2,1)S(1)}, bf16[4,24,896]{2,1,0:T(8,128)(2,1)S(1)}, u32[]{:S(2)}, u32[]{:S(2)}) collective-permute-start(bf16[4,24,896]{2,1,0:T(8,128)(2,1)S(1)} %collective-permute-done.5.refs_3_), channel_id=1, source_target_pairs={{0,1},{1,0},{2,3},{3,2},{4,5},{5,4},{6,7},{7,6},{8,9},{9,8},{10,11... | collective-permute-start | bytes 516104 | tf_op jit(solution)/shard_map/ppermute | solution.py:458
  44.1 1.4 collective-permute-start.8
  44.1 47.4 %copy-start.11 = (bf16[4,24,1536]{2,1,0:T(8,128)(2,1)}, bf16[4,24,1536]{2,1,0:T(8,128)(2,1)S(1)}, u32[]{:S(2)}) copy-start(bf16[4,24,1536]{2,1,0:T(8,128)(2,1)S(1)} %collective-permute-done.15.refs_3_) | copy-start | bytes 884740
  44.2 65.9 %collective-permute-start.16 = (bf16[4,24,1536]{2,1,0:T(8,128)(2,1)S(1)}, bf16[4,24,1536]{2,1,0:T(8,128)(2,1)S(1)}, u32[]{:S(2)}, u32[]{:S(2)}) collective-permute-start(bf16[4,24,1536]{2,1,0:T(8,128)(2,1)S(1)} %pad_maximum_fusion.refs_0_), channel_id=1, source_target_pairs={{0,1},{1,0},{2,3},{3,2},{4,5},{5,4},{6,7},{7,6},{8,9},{9,8},{10,11... | collective-permute-start | bytes 884744 | tf_op jit(solution)/shard_map/ppermute | solution.py:458
  44.7 46.9 %copy-start.12 = (bf16[4,24,1536]{2,1,0:T(8,128)(2,1)}, bf16[4,24,1536]{2,1,0:T(8,128)(2,1)S(1)}, u32[]{:S(2)}) copy-start(bf16[4,24,1536]{2,1,0:T(8,128)(2,1)S(1)} %collective-permute-done.14.refs_2_) | copy-start | bytes 884740
  44.7 65.5 %collective-permute-start.19 = (bf16[4,24,1536]{2,1,0:T(8,128)(2,1)S(1)}, bf16[4,24,1536]{2,1,0:T(8,128)(2,1)S(1)}, u32[]{:S(2)}, u32[]{:S(2)}) collective-permute-start(bf16[4,24,1536]{2,1,0:T(8,128)(2,1)S(1)} %collective-permute-done.15.refs_3_), channel_id=1, source_target_pairs={{0,1},{1,0},{2,3},{3,2},{4,5},{5,4},{6,7},{7,6},{8,9},{9,8},{10,11... | collective-permute-start | bytes 884744 | tf_op jit(solution)/shard_map/ppermute | solution.py:458
  44.7 46.8 %copy-start.13 = (bf16[4,24,1536]{2,1,0:T(8,128)(2,1)}, bf16[4,24,1536]{2,1,0:T(8,128)(2,1)S(1)}, u32[]{:S(2)}) copy-start(bf16[4,24,1536]{2,1,0:T(8,128)(2,1)S(1)} %collective-permute-done.13.refs_1_) | copy-start | bytes 884740
  44.8 65.4 %collective-permute-start.18 = (bf16[4,24,1536]{2,1,0:T(8,128)(2,1)S(1)}, bf16[4,24,1536]{2,1,0:T(8,128)(2,1)S(1)}, u32[]{:S(2)}, u32[]{:S(2)}) collective-permute-start(bf16[4,24,1536]{2,1,0:T(8,128)(2,1)S(1)} %collective-permute-done.14.refs_2_), channel_id=1, source_target_pairs={{0,1},{1,0},{2,3},{3,2},{4,5},{5,4},{6,7},{7,6},{8,9},{9,8},{10,11... | collective-permute-start | bytes 884744 | tf_op jit(solution)/shard_map/ppermute | solution.py:458
  45.2 65.0 %collective-permute-start.17 = (bf16[4,24,1536]{2,1,0:T(8,128)(2,1)S(1)}, bf16[4,24,1536]{2,1,0:T(8,128)(2,1)S(1)}, u32[]{:S(2)}, u32[]{:S(2)}) collective-permute-start(bf16[4,24,1536]{2,1,0:T(8,128)(2,1)S(1)} %collective-permute-done.13.refs_1_), channel_id=1, source_target_pairs={{0,1},{1,0},{2,3},{3,2},{4,5},{5,4},{6,7},{7,6},{8,9},{9,8},{10,11... | collective-permute-start | bytes 884744 | tf_op jit(solution)/shard_map/ppermute | solution.py:458
  46.2 1.5 collective-permute-start.7
  212.3 39.1 %collective-permute-start.29 = (bf16[384,1536]{1,0:T(8,128)(2,1)}, bf16[384,1536]{1,0:T(8,128)(2,1)S(1)}, u32[]{:S(2)}, u32[]{:S(2)}) collective-permute-start(bf16[384,1536]{1,0:T(8,128)(2,1)} %get-tuple-element.85), channel_id=1, source_target_pairs={{0,1},{1,0},{2,3},{3,2},{4,5},{5,4},{6,7},{7,6},{8,9},{9,8},{10,11... | collective-permute-start | bytes 3538952 | tf_op jit(solution)/shard_map/ppermute | solution.py:458
  212.6 29.8 %copy-start.8 = (bf16[197,8,384]{2,1,0:T(8,128)(2,1)S(1)}, bf16[197,8,384]{2,1,0:T(8,128)(2,1)}, u32[]{:S(2)}) copy-start(bf16[197,8,384]{2,1,0:T(8,128)(2,1)} %get-tuple-element.57.own) | copy-start | bytes 3631108
  241.9 2.4 collective-permute-start.22
  242.1 44.7 %collective-permute-start.21 = (bf16[197,8,384]{2,1,0:T(8,128)(2,1)}, bf16[197,8,384]{2,1,0:T(8,128)(2,1)}, u32[]{:S(2)}, u32[]{:S(2)}) collective-permute-start(bf16[197,8,384]{2,1,0:T(8,128)(2,1)} %get-tuple-element.65.own), channel_id=1, source_target_pairs={{0,1},{1,0},{2,3},{3,2},{4,5},{5,4},{6,7},{7,6},{8,9},{9,8},{10,11... | collective-permute-start | bytes 3631112 | tf_op jit(solution)/shard_map/ppermute | solution.py:458
  242.4 119.5 %collective-permute-start.20 = (bf16[197,8,384]{2,1,0:T(8,128)(2,1)S(1)}, bf16[197,8,384]{2,1,0:T(8,128)(2,1)}, u32[]{:S(2)}, u32[]{:S(2)}) collective-permute-start(bf16[197,8,384]{2,1,0:T(8,128)(2,1)S(1)} %copy-done.8), channel_id=1, source_target_pairs={{0,1},{1,0},{2,3},{3,2},{4,5},{5,4},{6,7},{7,6},{8,9},{9,8},{10,11... | collective-permute-start | bytes 3631112 | tf_op jit(solution)/shard_map/ppermute | solution.py:458
  249.3 8.3 %collective-permute-start.23 = (bf16[4,24,896]{2,1,0:T(8,128)(2,1)}, bf16[4,24,896]{2,1,0:T(8,128)(2,1)S(1)}, u32[]{:S(2)}, u32[]{:S(2)}) collective-permute-start(bf16[4,24,896]{2,1,0:T(8,128)(2,1)} %get-tuple-element.69), channel_id=1, source_target_pairs={{0,2},{2,0},{4,6},{6,4},{8,10},{10,8},{12,14},{14,12},{16,18},{18,... | collective-permute-start | bytes 516104 | tf_op jit(solution)/shard_map/ppermute | solution.py:454
  250.9 10.1 %collective-permute-start.24 = (bf16[4,24,896]{2,1,0:T(8,128)(2,1)}, bf16[4,24,896]{2,1,0:T(8,128)(2,1)S(1)}, u32[]{:S(2)}, u32[]{:S(2)}) collective-permute-start(bf16[4,24,896]{2,1,0:T(8,128)(2,1)} %get-tuple-element.70), channel_id=1, source_target_pairs={{0,4},{2,6},{4,0},{6,2},{8,12},{10,14},{12,8},{14,10},{16,20},{18,... | collective-permute-start | bytes 516104 | tf_op jit(solution)/shard_map/ppermute | solution.py:454
  251.4 10.2 %collective-permute-start.25 = (bf16[4,24,896]{2,1,0:T(8,128)(2,1)}, bf16[4,24,896]{2,1,0:T(8,128)(2,1)S(1)}, u32[]{:S(2)}, u32[]{:S(2)}) collective-permute-start(bf16[4,24,896]{2,1,0:T(8,128)(2,1)} %get-tuple-element.71), channel_id=1, source_target_pairs={{0,6},{2,4},{4,2},{6,0},{8,14},{10,12},{12,10},{14,8},{16,22},{18,... | collective-permute-start | bytes 516104 | tf_op jit(solution)/shard_map/ppermute | solution.py:454
  257.7 5.4 %copy-start.5 = (bf16[4,24,896]{2,1,0:T(8,128)(2,1)}, bf16[4,24,896]{2,1,0:T(8,128)(2,1)S(1)}, u32[]{:S(2)}) copy-start(bf16[4,24,896]{2,1,0:T(8,128)(2,1)S(1)} %collective-permute-done.23.refs_4_.refs_5_.refs_6_.refs_7_) | copy-start | bytes 516100
  257.7 10.2 %collective-permute-start.30 = (bf16[4,24,1536]{2,1,0:T(8,128)(2,1)}, bf16[4,24,1536]{2,1,0:T(8,128)(2,1)S(1)}, u32[]{:S(2)}, u32[]{:S(2)}) collective-permute-start(bf16[4,24,1536]{2,1,0:T(8,128)(2,1)} %get-tuple-element.87), channel_id=1, source_target_pairs={{0,2},{2,0},{4,6},{6,4},{8,10},{10,8},{12,14},{14,12},{16,18},{18,... | collective-permute-start | bytes 884744 | tf_op jit(solution)/shard_map/ppermute | solution.py:454
  261.0 13.3 %collective-permute-start.31 = (bf16[4,24,1536]{2,1,0:T(8,128)(2,1)}, bf16[4,24,1536]{2,1,0:T(8,128)(2,1)S(1)}, u32[]{:S(2)}, u32[]{:S(2)}) collective-permute-start(bf16[4,24,1536]{2,1,0:T(8,128)(2,1)} %get-tuple-element.88), channel_id=1, source_target_pairs={{0,4},{2,6},{4,0},{6,2},{8,12},{10,14},{12,8},{14,10},{16,20},{18,... | collective-permute-start | bytes 884744 | tf_op jit(solution)/shard_map/ppermute | solution.py:454
  261.6 14.7 %collective-permute-start.32 = (bf16[4,24,1536]{2,1,0:T(8,128)(2,1)}, bf16[4,24,1536]{2,1,0:T(8,128)(2,1)S(1)}, u32[]{:S(2)}, u32[]{:S(2)}) collective-permute-start(bf16[4,24,1536]{2,1,0:T(8,128)(2,1)} %get-tuple-element.89), channel_id=1, source_target_pairs={{0,6},{2,4},{4,2},{6,0},{8,14},{10,12},{12,10},{14,8},{16,22},{18,... | collective-permute-start | bytes 884744 | tf_op jit(solution)/shard_map/ppermute | solution.py:454
  267.8 9.9 %copy-start.2 = (bf16[4,24,1536]{2,1,0:T(8,128)(2,1)}, bf16[4,24,1536]{2,1,0:T(8,128)(2,1)S(1)}, u32[]{:S(2)}) copy-start(bf16[4,24,1536]{2,1,0:T(8,128)(2,1)S(1)} %collective-permute-done.30.refs_4_.refs_5_.refs_6_.refs_7_) | copy-start | bytes 884740
  267.9 12.8 %collective-permute-start.26 = (bf16[1,24,896]{2,1,0:T(8,128)(2,1)}, bf16[1,24,896]{2,1,0:T(8,128)(2,1)S(1)}, u32[]{:S(2)}, u32[]{:S(2)}) collective-permute-start(bf16[1,24,896]{2,1,0:T(8,128)(2,1)} %get-tuple-element.73), channel_id=1, source_target_pairs={{0,8},{2,10},{4,12},{6,14},{8,0},{10,2},{12,4},{14,6},{16,24},{18,... | collective-permute-start | bytes 129032 | tf_op jit(solution)/shard_map/ppermute | solution.py:454
  274.3 7.6 %collective-permute-start.27 = (bf16[1,24,896]{2,1,0:T(8,128)(2,1)}, bf16[1,24,896]{2,1,0:T(8,128)(2,1)S(1)}, u32[]{:S(2)}, u32[]{:S(2)}) collective-permute-start(bf16[1,24,896]{2,1,0:T(8,128)(2,1)} %get-tuple-element.74), channel_id=1, source_target_pairs={{0,16},{2,18},{4,20},{6,22},{8,24},{10,26},{12,28},{14,30},{16,0},... | collective-permute-start | bytes 129032 | tf_op jit(solution)/shard_map/ppermute | solution.py:454
  276.2 7.4 %collective-permute-start.28 = (bf16[1,24,896]{2,1,0:T(8,128)(2,1)}, bf16[1,24,896]{2,1,0:T(8,128)(2,1)S(1)}, u32[]{:S(2)}, u32[]{:S(2)}) collective-permute-start(bf16[1,24,896]{2,1,0:T(8,128)(2,1)} %get-tuple-element.75), channel_id=1, source_target_pairs={{0,24},{2,26},{4,28},{6,30},{8,16},{10,18},{12,20},{14,22},{16,8},... | collective-permute-start | bytes 129032 | tf_op jit(solution)/shard_map/ppermute | solution.py:454
  280.7 4.5 %copy-start.27 = (bf16[1,24,896]{2,1,0:T(8,128)(2,1)}, bf16[1,24,896]{2,1,0:T(8,128)(2,1)S(1)}, u32[]{:S(2)}) copy-start(bf16[1,24,896]{2,1,0:T(8,128)(2,1)S(1)} %collective-permute-done.26.refs_1_) | copy-start | bytes 129028
  280.7 156.4 %collective-permute-start.33 = (bf16[1,24,1536]{2,1,0:T(8,128)(2,1)}, bf16[1,24,1536]{2,1,0:T(8,128)(2,1)S(1)}, u32[]{:S(2)}, u32[]{:S(2)}) collective-permute-start(bf16[1,24,1536]{2,1,0:T(8,128)(2,1)} %get-tuple-element.91), channel_id=1, source_target_pairs={{0,8},{2,10},{4,12},{6,14},{8,0},{10,2},{12,4},{14,6},{16,24},{18,... | collective-permute-start | bytes 221192 | tf_op jit(solution)/shard_map/ppermute | solution.py:454
  281.9 155.2 %collective-permute-start.34 = (bf16[1,24,1536]{2,1,0:T(8,128)(2,1)}, bf16[1,24,1536]{2,1,0:T(8,128)(2,1)S(1)}, u32[]{:S(2)}, u32[]{:S(2)}) collective-permute-start(bf16[1,24,1536]{2,1,0:T(8,128)(2,1)} %get-tuple-element.92), channel_id=1, source_target_pairs={{0,16},{2,18},{4,20},{6,22},{8,24},{10,26},{12,28},{14,30},{16,0},... | collective-permute-start | bytes 221192 | tf_op jit(solution)/shard_map/ppermute | solution.py:454
  283.6 153.5 %collective-permute-start.35 = (bf16[1,24,1536]{2,1,0:T(8,128)(2,1)}, bf16[1,24,1536]{2,1,0:T(8,128)(2,1)S(1)}, u32[]{:S(2)}, u32[]{:S(2)}) collective-permute-start(bf16[1,24,1536]{2,1,0:T(8,128)(2,1)} %get-tuple-element.93), channel_id=1, source_target_pairs={{0,24},{2,26},{4,28},{6,30},{8,16},{10,18},{12,20},{14,22},{16,8},... | collective-permute-start | bytes 221192 | tf_op jit(solution)/shard_map/ppermute | solution.py:454
  (18 other events, 27.8 us)
where the time goes:
time: 440 us; the launch traced here: 439 us
  Pallas kernels  360 us (82%)
  starting transfers between devices  36.9 us (8%)
  waiting for transfers between devices  27.6 us (6%)
  local copies, waits for them, and re-layouts  11.8 us (3%)
    pallas_call x2, Pallas kernels, join(): pl.pallas_call(kernel, in_specs=[pl.BlockSpec(memory_space=pltpu.SMEM), a...  150 us
    pallas_call x2, Pallas kernels, assemble(): pl.pallas_call(kernel, in_specs=[pl.BlockSpec(memory_space=pltpu.SMEM)] +...  117 us
    ppermute x24, starting transfers between devices, hop(): return lax.ppermute(array, 'shard', [(i, i ^ offset) for i in range(count)])  34.5 us
    pallas_call x1, Pallas kernels, call_attention_backward(): pl.pallas_call(functools.partial(attention_backward, rows), grid_spec=plt...  29.3 us
    pallas_call x1, Pallas kernels, call_feed_forward(): pl.pallas_call(functools.partial(feed_forward, rows, chunk, length), grid...  26.9 us
    ppermute x24, waiting for transfers between devices, hop(): return lax.ppermute(array, 'shard', [(i, i ^ offset) for i in range(count)])  25.6 us
    pallas_call x1, Pallas kernels, call_attention_forward(): pl.pallas_call(functools.partial(attention_forward, rows), grid_spec=pltp...  18.5 us
    pallas_call x4, Pallas kernels, combine(): pl.pallas_call(kernel, grid_spec=pltpu.PrefetchScalarGridSpec(num_scalar_...  14.4 us
  transfers between devices with their start and end apart: 36, of which 11 were waited for; matrix products, arithmetic and copies ran while one was open for 0% of the time, Pallas kernels for 59%

commit v1 on v0

--- a/solution.py
+++ b/solution.py
@@ -13,7 +13,8 @@
 LOW = jnp.bfloat16
 WIDE = jnp.float32
 SMALL = 128
-VMEM_LIMIT = 60 * 1024 * 1024
+VMEM_LIMIT = 32 * 1024 * 1024
+SMALL_LIMIT = 16 * 1024 * 1024
 
 
 def nn(a, b):
@@ -471,70 +472,76 @@
 
 def assemble(scalars, got, marks, count):
     arrays = got + [swap(g) for g in got]
-    places = [(half, a, b, mark) for half in range(2) for a, line in enumerate(marks) for b, mark in enumerate(line)]
+    radix = len(got)
+    blocks, rows, columns = got[0].shape
+
+    def high_mark(i):
+        found = jnp.int32(0)
+        for b, mark in enumerate(marks[0]):
+            found = jnp.where(i == b, jnp.int32(mark), found)
+        return found
 
     def kernel(scalars, *refs):
-        ins, out, sems = refs[: len(arrays)], refs[-2], refs[-1]
-        copies = []
-        for at, (half, a, b, mark) in enumerate(places):
-            owner = lax.bitwise_xor(scalars[2], mark)
-            source = ins[half * len(got) + a].at[b]
-            copies.append(pltpu.make_async_copy(source, out.at[half, owner], sems.at[at]))
-        for copy in copies:
-            copy.start()
-        for copy in copies:
-            copy.wait()
-
-    shape = (2, count) + got[0].shape[1:]
-    anywhere = pl.BlockSpec(memory_space=pl.ANY)
-    return pl.pallas_call(
-        kernel,
-        in_specs=[pl.BlockSpec(memory_space=pltpu.SMEM)] + [anywhere] * len(arrays),
-        out_specs=anywhere,
-        scratch_shapes=[pltpu.SemaphoreType.DMA((len(places),))],
-        out_shape=jax.ShapeDtypeStruct(shape, LOW),
-        name="assemble",
-    )(scalars, *arrays)
-
-
-def combine(scalars, arrays, stride, radix):
-    blocks, rows, columns = arrays[0].shape
-    high = blocks // radix
-
-    def kernel(scalars, *refs):
-        outs = refs[len(arrays) * radix :]
-        for k in range(radix):
-            total = None
-            for a in range(len(arrays)):
-                value = refs[a * radix + k][0].astype(WIDE)
-                total = value if total is None else total + value
-            outs[k][0] = total.astype(outs[k].dtype)
-
-    def block(k):
-        def index(i, s):
-            return (i * radix + (lax.rem(lax.div(s[2], stride), radix) ^ k), 0, 0)
-
-        return pl.BlockSpec((1, rows, columns), index)
+        out = refs[-1]
+        for half in range(2):
+            for a in range(radix):
+                place = lax.bitwise_xor(lax.rem(scalars[2], radix), a)
+                out[half, pl.ds(place, 1)] = refs[half * radix + a][...]
 
     return pl.pallas_call(
         kernel,
         grid_spec=pltpu.PrefetchScalarGridSpec(
             num_scalar_prefetch=1,
-            grid=(high,),
-            in_specs=[block(k) for _ in arrays for k in range(radix)],
-            out_specs=[pl.BlockSpec((1, rows, columns), lambda i, s: (i, 0, 0))] * radix,
+            grid=(blocks,),
+            in_specs=[pl.BlockSpec((1, rows, columns), lambda i, s: (i, 0, 0))] * len(arrays),
+            out_specs=pl.BlockSpec(
+                (2, radix, rows, columns), lambda i, s: (0, lax.div(lax.bitwise_xor(s[2], high_mark(i)), radix), 0, 0)
+            ),
+        ),
+        out_shape=jax.ShapeDtypeStruct((2, count, rows, columns), LOW),
+        compiler_params=pltpu.CompilerParams(vmem_limit_bytes=SMALL_LIMIT),
+        name="assemble",
+    )(scalars, *arrays)
+
+
+def combine(scalars, arrays, stride, radix):
+    blocks, rows, columns = arrays[0].shape
+    high = blocks // radix
+    views = [a.reshape(high, radix, rows, columns) for a in arrays]
+
+    def kernel(scalars, *refs):
+        outs = refs[len(views) :]
+        digit = lax.rem(lax.div(scalars[2], stride), radix)
+        for k in range(radix):
+            for i in range(outs[0].shape[0]):
+                total = None
+                for ref in refs[: len(views)]:
+                    value = ref[i, lax.bitwise_xor(digit, k)].astype(WIDE)
+                    total = value if total is None else total + value
+                outs[k][i] = total.astype(outs[k].dtype)
+
+    step = max(1, high // 2)
+    return pl.pallas_call(
+        kernel,
+        grid_spec=pltpu.PrefetchScalarGridSpec(
+            num_scalar_prefetch=1,
+            grid=(high // step,),
+            in_specs=[pl.BlockSpec((step, radix, rows, columns), lambda i, s: (i, 0, 0, 0))] * len(views),
+            out_specs=[pl.BlockSpec((step, rows, columns), lambda i, s: (i, 0, 0))] * radix,
         ),
         out_shape=[jax.ShapeDtypeStruct((high, rows, columns), LOW if k else WIDE) for k in range(radix)],
+        compiler_params=pltpu.CompilerParams(vmem_limit_bytes=SMALL_LIMIT),
         name="combine",
-    )(scalars, *[a for a in arrays for _ in range(radix)])
-
-
-def scatter_rows(scalars, own, received, count):
-    arrays = [own, received]
-    for stride, radix in stages_of(count)[::-1]:
+    )(scalars, *views)
+
+
+def scatter_rows(scalars, arrays, count, levels, after=None):
+    for at, (stride, radix) in enumerate(levels):
         sums = combine(scalars, arrays, stride, radix)
+        if at == 0 and after is not None:
+            *sums, after = lax.optimization_barrier((*sums, after))
         arrays = [sums[0]] + [hop(sums[k], count, k * stride) for k in range(1, radix)]
-    return arrays
+    return (arrays, after) if after is not None else arrays
 
 
 def total_of(refs):
@@ -553,7 +560,8 @@
         refs[-1][...] = total[:, units:]
 
     return pl.pallas_call(
-        kernel, out_shape=[jax.ShapeDtypeStruct((rows, units), WIDE)] * 2, name="finish_second"
+        kernel, out_shape=[jax.ShapeDtypeStruct((rows, units), WIDE)] * 2,
+        compiler_params=pltpu.CompilerParams(vmem_limit_bytes=SMALL_LIMIT), name="finish_second"
     )(*arrays)
 
 
@@ -586,37 +594,64 @@
 
     shapes = [(3, rows, half), (rows, half)] + [(1, rows)] * 6 + [(2, 1, rows // 2), (1, per)]
     return pl.pallas_call(
-        kernel, out_shape=[jax.ShapeDtypeStruct(s, WIDE) for s in shapes], name="finish_first"
+        kernel, out_shape=[jax.ShapeDtypeStruct(s, WIDE) for s in shapes],
+        compiler_params=pltpu.CompilerParams(vmem_limit_bytes=SMALL_LIMIT), name="finish_first"
     )(*arrays)
 
 
-def join(scalars, array):
+def join(scalars, array, chunk=50):
     length, images, width = array.shape
     other = swap(array)
 
-    def kernel(scalars, own, other, out, sems):
-        here = pltpu.make_async_copy(own, out.at[:, scalars[0]], sems.at[0])
-        there = pltpu.make_async_copy(other, out.at[:, 1 - scalars[0]], sems.at[1])
-        here.start()
-        there.start()
-        here.wait()
-        there.wait()
-
-    anywhere = pl.BlockSpec(memory_space=pl.ANY)
+    def kernel(scalars, own, other, out):
+        out[:, pl.ds(scalars[0], 1)] = own[...][:, None]
+        out[:, pl.ds(1 - scalars[0], 1)] = other[...][:, None]
+
+    part = pl.BlockSpec((chunk, images, width), lambda i, s: (i, 0, 0))
     out = pl.pallas_call(
         kernel,
-        in_specs=[pl.BlockSpec(memory_space=pltpu.SMEM), anywhere, anywhere],
-        out_specs=anywhere,
-        scratch_shapes=[pltpu.SemaphoreType.DMA((2,))],
+        grid_spec=pltpu.PrefetchScalarGridSpec(
+            num_scalar_prefetch=1,
+            grid=(pl.cdiv(length, chunk),),
+            in_specs=[part, part],
+            out_specs=pl.BlockSpec((chunk, 2, images, width), lambda i, s: (i, 0, 0, 0)),
+        ),
         out_shape=jax.ShapeDtypeStruct((length, 2, images, width), array.dtype),
+        compiler_params=pltpu.CompilerParams(vmem_limit_bytes=SMALL_LIMIT),
         name="join",
     )(scalars, array, other)
     return out.reshape(length, 2 * images, width).transpose(1, 0, 2)
 
 
-def pack_small(columns):
-    block = jnp.stack(columns, axis=-1)
-    return jnp.pad(block, [(0, 0), (0, SMALL - block.shape[-1])])
+def pack(input_weight, output_t, expand, reduce_t, flat):
+    rows, half = output_t.shape
+    units = expand.shape[1]
+    vectors = flat.shape[0]
+
+    def kernel(w_in, w_out, w_expand, w_reduce, flat, first, second):
+        for i in range(3):
+            first[:, i * half : (i + 1) * half] = w_in[i]
+        first[:, 3 * half : 4 * half] = w_out[...]
+        row = lax.broadcasted_iota(jnp.int32, (rows, rows), 0)
+        lane = lax.broadcasted_iota(jnp.int32, (rows, rows), 1)
+        place = lax.broadcasted_iota(jnp.int32, (rows, SMALL), 1)
+        tiny = jnp.zeros((rows, SMALL), WIDE)
+        for j in range(vectors):
+            column = jnp.sum(jnp.where(row == lane, flat[j : j + 1], 0.0), 1, keepdims=True)
+            tiny = jnp.where(place == j, column, tiny)
+        first[:, 4 * half :] = tiny.astype(LOW)
+        second[:, :units] = w_expand[...]
+        second[:, units:] = w_reduce[...]
+
+    return pl.pallas_call(
+        kernel,
+        out_shape=[
+            jax.ShapeDtypeStruct((rows, 4 * half + SMALL), LOW),
+            jax.ShapeDtypeStruct((rows, 2 * units), LOW),
+        ],
+        compiler_params=pltpu.CompilerParams(vmem_limit_bytes=SMALL_LIMIT),
+        name="pack",
+    )(input_weight, output_t, expand, reduce_t, flat)
 
 
 def body(shards, tokens, image_counts, input_weight, query_value_bias, output_weight, output_bias, first_gain,
@@ -626,11 +661,10 @@
     width = rows * shards
     images = tokens.shape[0] // 2
     scalars = jnp.stack([lax.axis_index("tensor"), image_counts[0], lax.axis_index("shard")]).astype(jnp.int32)
-    small = pack_small(
-        [first_gain, first_shift, second_gain, second_shift, output_bias, reduce_bias, query_value_bias.reshape(-1)]
-        + list(expand_bias.reshape(-1, rows)))
-    first = jnp.concatenate([input_weight[0], input_weight[1], input_weight[2], output_weight.T, small], axis=1)
-    second = jnp.concatenate([expand_weight, reduce_weight.T], axis=1)
+    flat = jnp.concatenate(
+        [first_gain, first_shift, second_gain, second_shift, output_bias, reduce_bias, query_value_bias.reshape(-1),
+         expand_bias.reshape(-1)]).astype(WIDE).reshape(-1, rows)
+    first, second = pack(input_weight, output_weight.T, expand_weight, reduce_weight.T, flat)
     first = assemble(scalars, *gather_pieces(first, shards), shards).reshape(2, width, -1)
     second = assemble(scalars, *gather_pieces(second, shards), shards).reshape(2, width, -1)
     tokens = tokens.transpose(1, 0, 2)
@@ -638,14 +672,17 @@
     normed, qkv, probs, attended, middle, joined = call_attention_forward(rows, scalars, tokens, first, images)
     mixed, grad_middle, own, other, sums = call_feed_forward(rows, scalars, middle, cotangent, first, second, images)
 
-    def spread(own, other):
+    levels = stages_of(shards)[::-1]
+
+    def paired(own, other):
         shape = (shards, rows, -1)
-        return scatter_rows(scalars, own.reshape(shape), swap(other).reshape(shape), shards)
-
-    grad_expand, grad_reduce = finish_second(spread(own, other), units)
+        return [own.reshape(shape), swap(other).reshape(shape)]
+
+    arrays, grad_middle = scatter_rows(scalars, paired(own, other), shards, levels, grad_middle)
+    grad_expand, grad_reduce = finish_second(arrays, units)
     token_grad, own, other = call_attention_backward(
         rows, scalars, tokens, grad_middle, normed, qkv, probs, attended, joined, first, sums, images)
-    outs = finish_first(spread(own, other), half, units)
+    outs = finish_first(scatter_rows(scalars, paired(own, other), shards, levels), half, units)
     gains = [o.reshape(rows) for o in outs[2:8]]
     return (
         join(scalars, mixed),

time: 440 us -> 169 us (0.38)
  Pallas kernels: 360 us -> 75.5 us
  waiting for transfers between devices: 27.6 us -> 42.4 us
    pallas_call x4 -> x5, Pallas kernels: 268 us -> 8.65 us  [the longest x2 5.03 us: join(): pl.pallas_call(kernel, grid_spec=pltpu.PrefetchScalarGridSpec(num_scalar_...]
    ppermute x24, waiting for transfers between devices: 25.6 us -> 39 us  [hop(): return lax.ppermute(array, 'shard', [(i, i ^ offset) for i in range(count)])]
    pallas_call x4, Pallas kernels: 14.4 us -> 2.88 us  [combine(): pl.pallas_call(kernel, grid_spec=pltpu.PrefetchScalarGridSpec(num_scalar_...]
    another operation x11 -> x0, local copies, waits for them, and re-layouts: 6.33 us -> none  [pack_small(): block = jnp.stack(columns, axis=-1)]
    pallas_call x1, Pallas kernels: 29.3 us -> 24.1 us  [call_attention_backward(): pl.pallas_call(functools.partial(attention_backward, rows), grid_spec=plt...]
    unnamed x60 -> x20, local copies, waits for them, and re-layouts: 3.96 us -> 9.13 us
  transfers between devices with their start and end apart: 36 -> 36, of which waited for: 11 -> 13; matrix products, arithmetic and copies ran while one was open for 0% -> 0% of each run, Pallas kernels for 59% -> 29%
where the time goes in v1:
time: 169 us; the launch traced here: 168 us
  Pallas kernels  75.5 us (45%)
  waiting for transfers between devices  42.4 us (25%)
  starting transfers between devices  33.7 us (20%)
  local copies, waits for them, and re-layouts  14.7 us (9%)
    ppermute x24, waiting for transfers between devices, hop(): return lax.ppermute(array, 'shard', [(i, i ^ offset) for i in range(count)])  39 us
    ppermute x24, starting transfers between devices, hop(): return lax.ppermute(array, 'shard', [(i, i ^ offset) for i in range(count)])  31.2 us
    pallas_call x1, Pallas kernels, call_attention_backward(): pl.pallas_call(functools.partial(attention_backward, rows), grid_spec=plt...  24.1 us
    pallas_call x1, Pallas kernels, call_feed_forward(): pl.pallas_call(functools.partial(feed_forward, rows, chunk, length), grid...  23.5 us
    pallas_call x1, Pallas kernels, call_attention_forward(): pl.pallas_call(functools.partial(attention_forward, rows), grid_spec=pltp...  15 us
    unnamed x20, local copies, waits for them, and re-layouts  9.13 us
    pallas_call x2, Pallas kernels, join(): pl.pallas_call(kernel, grid_spec=pltpu.PrefetchScalarGridSpec(num_scalar_...  5.03 us
    concatenate x1, local copies, waits for them, and re-layouts, body(): jnp.concatenate([first_gain, first_shift, second_gain, second_shift, outp...  4.76 us
  transfers between devices with their start and end apart: 36, of which 13 were waited for; matrix products, arithmetic and copies ran while one was open for 0% of the time, Pallas kernels for 29%

profile of v1, /device:TPU:0, one launch (start us, length us, event | category | flops | bytes accessed | tf_op | source)
XLA Modules:
  0.0 167.9 jit_solution(5602203604277907324)
XLA Ops:
  0.6 0.7 reshape.92
  1.4 4.8 %concatenate.9 = bf16[216]{0:T(256)(128)(2,1)S(1)} concatenate(bf16[24]{0:T(256)(128)(2,1)} %param.21, bf16[24]{0:T(256)(128)(2,1)} %param.22, bf16[24]{0:T(256)(128)(2,1)} %param.23, bf16[24]{0:T(256)(128)(2,1)} %param.24, bf16[24]{0:T(256)(128)(2,1)} %param.20, bf16[24]{0:T(256)(128)(2,1)} %param.28, bf16[24]{0:T(256)(128)(2,1)S(1)} %reshape.92, bf16[48]{0:T(256)(128)(2,1)} %bitcast.70), dimensions={0} | concatenate | bytes 864 | tf_op jit(solution)/shard_map/concatenate | solution.py:664
  6.2 0.8 copy-done.6
  7.0 0.8 copy-done.7
  7.8 0.8 copy-done.8
  8.5 0.7 copy-done.9
  9.4 5.1 %collective-permute-start.2 = (bf16[1,24,896]{2,1,0:T(8,128)(2,1)S(1)}, bf16[1,24,896]{2,1,0:T(8,128)(2,1)S(1)}, u32[]{:S(2)}, u32[]{:S(2)}) collective-permute-start(bf16[1,24,896]{2,1,0:T(8,128)(2,1)S(1)} %bitcast.62), channel_id=1, source_target_pairs={{0,24},{2,26},{4,28},{6,30},{8,16},{10,18},{12,20},{14,22},{16,8},... | collective-permute-start | bytes 129032 | tf_op jit(solution)/shard_map/ppermute | solution.py:455
  15.1 3.7 %collective-permute-start.12 = (bf16[1,24,1536]{2,1,0:T(8,128)(2,1)S(1)}, bf16[1,24,1536]{2,1,0:T(8,128)(2,1)S(1)}, u32[]{:S(2)}, u32[]{:S(2)}) collective-permute-start(bf16[1,24,1536]{2,1,0:T(8,128)(2,1)S(1)} %bitcast.58), channel_id=1, source_target_pairs={{0,24},{2,26},{4,28},{6,30},{8,16},{10,18},{12,20},{14,22},{16,8},... | collective-permute-start | bytes 221192 | tf_op jit(solution)/shard_map/ppermute | solution.py:455
  18.9 0.6 collective-permute-start.10
  19.5 3.1 %collective-permute-done.1 = bf16[1,24,896]{2,1,0:T(8,128)(2,1)S(1)} collective-permute-done((bf16[1,24,896]{2,1,0:T(8,128)(2,1)S(1)}, bf16[1,24,896]{2,1,0:T(8,128)(2,1)S(1)}, u32[]{:S(2)}, u32[]{:S(2)}) %collective-permute-start.1) | collective-permute-done | bytes 43040 | tf_op jit(solution)/shard_map/ppermute | solution.py:455
  22.7 2.5 %collective-permute-start.5 = (bf16[4,24,896]{2,1,0:T(8,128)(2,1)S(1)}, bf16[4,24,896]{2,1,0:T(8,128)(2,1)S(1)}, u32[]{:S(2)}, u32[]{:S(2)}) collective-permute-start(bf16[4,24,896]{2,1,0:T(8,128)(2,1)S(1)} %pad_maximum_fusion.1.refs_0_), channel_id=1, source_target_pairs={{0,6},{2,4},{4,2},{6,0},{8,14},{10,12},{12,10},{14,8},{16,22},{18,... | collective-permute-start | bytes 516104 | tf_op jit(solution)/shard_map/ppermute | solution.py:455
  25.8 2.0 %collective-permute-start.15 = (bf16[4,24,1536]{2,1,0:T(8,128)(2,1)S(1)}, bf16[4,24,1536]{2,1,0:T(8,128)(2,1)S(1)}, u32[]{:S(2)}, u32[]{:S(2)}) collective-permute-start(bf16[4,24,1536]{2,1,0:T(8,128)(2,1)S(1)} %pad_maximum_fusion.refs_0_), channel_id=1, source_target_pairs={{0,6},{2,4},{4,2},{6,0},{8,14},{10,12},{12,10},{14,8},{16,22},{18,... | collective-permute-start | bytes 884744 | tf_op jit(solution)/shard_map/ppermute | solution.py:455
  28.3 1.1 collective-permute-start.13
  29.4 1.7 %collective-permute-done.5.refs_3_ = bf16[4,24,896]{2,1,0:T(8,128)(2,1)S(1)} collective-permute-done((bf16[4,24,896]{2,1,0:T(8,128)(2,1)S(1)}, bf16[4,24,896]{2,1,0:T(8,128)(2,1)S(1)}, u32[]{:S(2)}, u32[]{:S(2)}) %collective-permute-start.5) | collective-permute-done | bytes 172064 | tf_op jit(solution)/shard_map/ppermute | solution.py:455
  31.1 1.5 collective-permute-start.3
  32.6 7.9 %collective-permute-done.4.refs_2_ = bf16[4,24,896]{2,1,0:T(8,128)(2,1)S(1)} collective-permute-done((bf16[4,24,896]{2,1,0:T(8,128)(2,1)S(1)}, bf16[4,24,896]{2,1,0:T(8,128)(2,1)S(1)}, u32[]{:S(2)}, u32[]{:S(2)}) %collective-permute-start.4) | collective-permute-done | bytes 172064 | tf_op jit(solution)/shard_map/ppermute | solution.py:455
  40.5 6.3 %collective-permute-done.3.refs_1_ = bf16[4,24,896]{2,1,0:T(8,128)(2,1)S(1)} collective-permute-done((bf16[4,24,896]{2,1,0:T(8,128)(2,1)S(1)}, bf16[4,24,896]{2,1,0:T(8,128)(2,1)S(1)}, u32[]{:S(2)}, u32[]{:S(2)}) %collective-permute-start.3) | collective-permute-done | bytes 172064 | tf_op jit(solution)/shard_map/ppermute | solution.py:455
  48.3 0.7 copy-done.4
  49.8 0.7 collective-permute-done.7.refs_5_
  50.5 1.0 copy-done.5
  51.4 2.4 %assemble.2 = bf16[2,16,24,896]{3,2,1,0:T(8,128)(2,1)S(1)} custom-call(s32[3]{0:T(128)S(1)} %pad_add_fusion.scalars, bf16[4,24,896]{2,1,0:T(8,128)(2,1)S(1)} %pad_maximum_fusion.1.refs_0_, bf16[4,24,896]{2,1,0:T(8,128)(2,1)S(1)} %collective-permute-done.3.refs_1_, bf16[4,24,896]{2,1,0:T(8,128)(2,1)S(1)} %collective-permute-done.4.refs_2_, ...), custom_call_target="tpu_custom_call" | custom-call | tf_op jit(solution)/shard_map/assemble/pallas_call | solution.py:491
  53.9 15.0 %attention_forward.1 = (bf16[8,208,384]{2,1,0:T(8,128)(2,1)S(1)}, bf16[8,208,1152]{2,1,0:T(8,128)(2,1)S(1)}, bf16[8,6,208,208]{3,2,1,0:T(8,128)(2,1)S(1)}, bf16[...) custom-call(s32[3]{0:T(128)S(1)} %pad_add_fusion.scalars, ...), custom_call_target="tpu_custom_call" | custom-call | tf_op jit(solution)/shard_map/attention_forward/pallas_call | solution.py:152
  68.9 1.8 %copy-done.1 = bf16[8,208,1152]{2,1,0:T(8,128)(2,1)} copy-done((bf16[8,208,1152]{2,1,0:T(8,128)(2,1)}, bf16[8,208,1152]{2,1,0:T(8,128)(2,1)S(1)}, u32[]{:S(2)}) %copy-start.1) | copy-done | bytes 3833880
  70.7 1.1 assemble.3
  72.4 23.5 %feed_forward.1 = (bf16[197,8,384]{2,1,0:T(8,128)(2,1)S(1)}, f32[3,1584,128]{2,1,0:T(8,128)S(1)}, f32[384,1536]{1,0:T(8,128)S(1)}, bf16[384,1536]{1,0:T(8,128)(2,1)S(1)}, f32[8,768]{1,0:T(8,128)S(1)}) custom-call(s32[3]{0:T(128)S(1)} %pad_add_fusion.scalars, f32[3,1584,128]{2,1,0:T(8,128)S(1)} %get-tuple-element.64.middle, ...), custom_call_target="tpu_custom_call" | custom-call | tf_op jit(solution)/shard_map/feed_forward/pallas_call | solution.py:257
  96.5 2.3 %collective-permute-done.21 = bf16[384,1536]{1,0:T(8,128)(2,1)S(1)} collective-permute-done((bf16[384,1536]{1,0:T(8,128)(2,1)S(1)}, bf16[384,1536]{1,0:T(8,128)(2,1)S(1)}, u32[]{:S(2)}, u32[]{:S(2)}) %collective-permute-start.21) | collective-permute-done | bytes 1179680 | tf_op jit(solution)/shard_map/ppermute | solution.py:459
  98.8 0.8 combine.4
  99.6 2.1 %copy-done.2 = bf16[8,208,1152]{2,1,0:T(8,128)(2,1)S(1)} copy-done((bf16[8,208,1152]{2,1,0:T(8,128)(2,1)S(1)}, bf16[8,208,1152]{2,1,0:T(8,128)(2,1)}, u32[]{:S(2)}) %copy-start.2) | copy-done | bytes 3833880
  101.7 24.1 %attention_backward.1 = (bf16[197,8,384]{2,1,0:T(8,128)(2,1)S(1)}, f32[384,896]{1,0:T(8,128)S(1)}, bf16[384,896]{1,0:T(8,128)(2,1)S(1)}) custom-call(s32[3]{0:T(128)S(1)} %pad_add_fusion.scalars, bf16[197,16,384]{2,1,0:T(8,128)(2,1)S(1)} %bitcast.43, f32[3,1584,128]{2,1,0:T(8,128)S(1)} %get-tuple-element.74.grad_middle, ...), custom_call_target="tpu_custom_call" | custom-call | tf_op jit(solution)/shard_map/attention_backward/pallas_call | solution.py:406
  126.4 1.5 collective-permute-start.30
  128.4 1.5 collective-permute-start.32
  129.9 0.7 combine.5
  130.6 5.6 %collective-permute-done.30 = bf16[4,24,1536]{2,1,0:T(8,128)(2,1)S(1)} collective-permute-done((bf16[4,24,1536]{2,1,0:T(8,128)(2,1)S(1)}, bf16[4,24,1536]{2,1,0:T(8,128)(2,1)S(1)}, u32[]{:S(2)}, u32[]{:S(2)}) %collective-permute-start.30) | collective-permute-done | bytes 294944 | tf_op jit(solution)/shard_map/ppermute | solution.py:455
  136.3 1.5 collective-permute-start.24
  137.8 5.4 %collective-permute-done.31 = bf16[4,24,1536]{2,1,0:T(8,128)(2,1)S(1)} collective-permute-done((bf16[4,24,1536]{2,1,0:T(8,128)(2,1)S(1)}, bf16[4,24,1536]{2,1,0:T(8,128)(2,1)S(1)}, u32[]{:S(2)}, u32[]{:S(2)}) %collective-permute-start.31) | collective-permute-done | bytes 294944 | tf_op jit(solution)/shard_map/ppermute | solution.py:455
  143.2 1.9 %collective-permute-start.26 = (bf16[4,24,896]{2,1,0:T(8,128)(2,1)S(1)}, bf16[4,24,896]{2,1,0:T(8,128)(2,1)S(1)}, u32[]{:S(2)}, u32[]{:S(2)}) collective-permute-start(bf16[4,24,896]{2,1,0:T(8,128)(2,1)S(1)} %get-tuple-element.87), channel_id=1, source_target_pairs={{0,6},{2,4},{4,2},{6,0},{8,14},{10,12},{12,10},{14,8},{16,22},{18,... | collective-permute-start | bytes 516104 | tf_op jit(solution)/shard_map/ppermute | solution.py:455
  145.1 0.7 combine.7
  145.9 5.6 %collective-permute-done.25 = bf16[4,24,896]{2,1,0:T(8,128)(2,1)S(1)} collective-permute-done((bf16[4,24,896]{2,1,0:T(8,128)(2,1)S(1)}, bf16[4,24,896]{2,1,0:T(8,128)(2,1)S(1)}, u32[]{:S(2)}, u32[]{:S(2)}) %collective-permute-start.25) | collective-permute-done | bytes 172064 | tf_op jit(solution)/shard_map/ppermute | solution.py:455
  151.5 0.7 collective-permute-start.35
  152.9 2.9 %collective-permute-start.27 = (bf16[1,24,896]{2,1,0:T(8,128)(2,1)S(1)}, bf16[1,24,896]{2,1,0:T(8,128)(2,1)S(1)}, u32[]{:S(2)}, u32[]{:S(2)}) collective-permute-start(bf16[1,24,896]{2,1,0:T(8,128)(2,1)S(1)} %get-tuple-element.89), channel_id=1, source_target_pairs={{0,8},{2,10},{4,12},{6,14},{8,0},{10,2},{12,4},{14,6},{16,24},{18,... | collective-permute-start | bytes 129032 | tf_op jit(solution)/shard_map/ppermute | solution.py:455
  155.7 0.9 collective-permute-start.28
  156.7 2.2 %collective-permute-done.34.refs_2_ = bf16[1,24,1536]{2,1,0:T(8,128)(2,1)S(1)} collective-permute-done((bf16[1,24,1536]{2,1,0:T(8,128)(2,1)S(1)}, bf16[1,24,1536]{2,1,0:T(8,128)(2,1)S(1)}, u32[]{:S(2)}, u32[]{:S(2)}) %collective-permute-start.34) | collective-permute-done | bytes 73760 | tf_op jit(solution)/shard_map/ppermute | solution.py:455
  158.8 1.6 collective-permute-start.29
  160.4 2.5 %join.2 = bf16[197,2,8,384]{3,2,1,0:T(8,128)(2,1)} custom-call(s32[3]{0:T(128)S(1)} %pad_add_fusion.scalars, bf16[197,8,384]{2,1,0:T(8,128)(2,1)S(1)} %get-tuple-element.66.own, bf16[197,8,384]{2,1,0:T(8,128)(2,1)S(1)} %collective-permute-done.20.other), custom_call_target="tpu_custom_call" | custom-call | tf_op jit(solution)/shard_map/join/pallas_call | solution.py:611
  162.9 0.7 finish_second.1
  163.6 1.1 collective-permute-done.29.refs_3_
  164.6 0.7 finish_first.1
  165.4 2.5 %join.3 = bf16[197,2,8,384]{3,2,1,0:T(8,128)(2,1)} custom-call(s32[3]{0:T(128)S(1)} %pad_add_fusion.scalars, bf16[197,8,384]{2,1,0:T(8,128)(2,1)S(1)} %get-tuple-element.81.own, bf16[197,8,384]{2,1,0:T(8,128)(2,1)S(1)} %collective-permute-done.22.other), custom_call_target="tpu_custom_call" | custom-call | tf_op jit(solution)/shard_map/join/pallas_call | solution.py:611
  (64 shorter events, 6.7 us)
Async XLA Ops:
  6.2 0.8 copy-start.6
  7.0 0.8 copy-start.7
  7.8 0.8 copy-start.8
  8.5 0.7 copy-start.9
  9.4 9.5 %collective-permute-start.2 = (bf16[1,24,896]{2,1,0:T(8,128)(2,1)S(1)}, bf16[1,24,896]{2,1,0:T(8,128)(2,1)S(1)}, u32[]{:S(2)}, u32[]{:S(2)}) collective-permute-start(bf16[1,24,896]{2,1,0:T(8,128)(2,1)S(1)} %bitcast.62), channel_id=1, source_target_pairs={{0,24},{2,26},{4,28},{6,30},{8,16},{10,18},{12,20},{14,22},{16,8},... | collective-permute-start | bytes 129032 | tf_op jit(solution)/shard_map/ppermute | solution.py:455
  14.5 8.1 %collective-permute-start.1 = (bf16[1,24,896]{2,1,0:T(8,128)(2,1)S(1)}, bf16[1,24,896]{2,1,0:T(8,128)(2,1)S(1)}, u32[]{:S(2)}, u32[]{:S(2)}) collective-permute-start(bf16[1,24,896]{2,1,0:T(8,128)(2,1)S(1)} %bitcast.63), channel_id=1, source_target_pairs={{0,16},{2,18},{4,20},{6,22},{8,24},{10,26},{12,28},{14,30},{16,0},... | collective-permute-start | bytes 129032 | tf_op jit(solution)/shard_map/ppermute | solution.py:455
  14.5 8.1 %collective-permute-start = (bf16[1,24,896]{2,1,0:T(8,128)(2,1)S(1)}, bf16[1,24,896]{2,1,0:T(8,128)(2,1)S(1)}, u32[]{:S(2)}, u32[]{:S(2)}) collective-permute-start(bf16[1,24,896]{2,1,0:T(8,128)(2,1)S(1)} %bitcast.64), channel_id=1, source_target_pairs={{0,8},{2,10},{4,12},{6,14},{8,0},{10,2},{12,4},{14,6},{16,24},{18,... | collective-permute-start | bytes 129032 | tf_op jit(solution)/shard_map/ppermute | solution.py:455
  15.1 10.1 %collective-permute-start.12 = (bf16[1,24,1536]{2,1,0:T(8,128)(2,1)S(1)}, bf16[1,24,1536]{2,1,0:T(8,128)(2,1)S(1)}, u32[]{:S(2)}, u32[]{:S(2)}) collective-permute-start(bf16[1,24,1536]{2,1,0:T(8,128)(2,1)S(1)} %bitcast.58), channel_id=1, source_target_pairs={{0,24},{2,26},{4,28},{6,30},{8,16},{10,18},{12,20},{14,22},{16,8},... | collective-permute-start | bytes 221192 | tf_op jit(solution)/shard_map/ppermute | solution.py:455
  18.9 6.9 %collective-permute-start.11 = (bf16[1,24,1536]{2,1,0:T(8,128)(2,1)S(1)}, bf16[1,24,1536]{2,1,0:T(8,128)(2,1)S(1)}, u32[]{:S(2)}, u32[]{:S(2)}) collective-permute-start(bf16[1,24,1536]{2,1,0:T(8,128)(2,1)S(1)} %bitcast.59), channel_id=1, source_target_pairs={{0,16},{2,18},{4,20},{6,22},{8,24},{10,26},{12,28},{14,30},{16,0},... | collective-permute-start | bytes 221192 | tf_op jit(solution)/shard_map/ppermute | solution.py:455
  18.9 6.9 %collective-permute-start.10 = (bf16[1,24,1536]{2,1,0:T(8,128)(2,1)S(1)}, bf16[1,24,1536]{2,1,0:T(8,128)(2,1)S(1)}, u32[]{:S(2)}, u32[]{:S(2)}) collective-permute-start(bf16[1,24,1536]{2,1,0:T(8,128)(2,1)S(1)} %bitcast.60), channel_id=1, source_target_pairs={{0,8},{2,10},{4,12},{6,14},{8,0},{10,2},{12,4},{14,6},{16,24},{18,... | collective-permute-start | bytes 221192 | tf_op jit(solution)/shard_map/ppermute | solution.py:455
  22.7 5.7 %collective-permute-start.6 = (bf16[4,24,896]{2,1,0:T(8,128)(2,1)S(1)}, bf16[4,24,896]{2,1,0:T(8,128)(2,1)S(1)}, u32[]{:S(2)}, u32[]{:S(2)}) collective-permute-start(bf16[4,24,896]{2,1,0:T(8,128)(2,1)S(1)} %pad_maximum_fusion.1.refs_0_), channel_id=1, source_target_pairs={{0,1},{1,0},{2,3},{3,2},{4,5},{5,4},{6,7},{7,6},{8,9},{9,8},{10,11... | collective-permute-start | bytes 516104 | tf_op jit(solution)/shard_map/ppermute | solution.py:459
  22.7 8.3 %collective-permute-start.5 = (bf16[4,24,896]{2,1,0:T(8,128)(2,1)S(1)}, bf16[4,24,896]{2,1,0:T(8,128)(2,1)S(1)}, u32[]{:S(2)}, u32[]{:S(2)}) collective-permute-start(bf16[4,24,896]{2,1,0:T(8,128)(2,1)S(1)} %pad_maximum_fusion.1.refs_0_), channel_id=1, source_target_pairs={{0,6},{2,4},{4,2},{6,0},{8,14},{10,12},{12,10},{14,8},{16,22},{18,... | collective-permute-start | bytes 516104 | tf_op jit(solution)/shard_map/ppermute | solution.py:455
  25.3 15.2 %collective-permute-start.4 = (bf16[4,24,896]{2,1,0:T(8,128)(2,1)S(1)}, bf16[4,24,896]{2,1,0:T(8,128)(2,1)S(1)}, u32[]{:S(2)}, u32[]{:S(2)}) collective-permute-start(bf16[4,24,896]{2,1,0:T(8,128)(2,1)S(1)} %pad_maximum_fusion.1.refs_0_), channel_id=1, source_target_pairs={{0,4},{2,6},{4,0},{6,2},{8,12},{10,14},{12,8},{14,10},{16,20},{18,... | collective-permute-start | bytes 516104 | tf_op jit(solution)/shard_map/ppermute | solution.py:455
  25.8 21.0 %collective-permute-start.15 = (bf16[4,24,1536]{2,1,0:T(8,128)(2,1)S(1)}, bf16[4,24,1536]{2,1,0:T(8,128)(2,1)S(1)}, u32[]{:S(2)}, u32[]{:S(2)}) collective-permute-start(bf16[4,24,1536]{2,1,0:T(8,128)(2,1)S(1)} %pad_maximum_fusion.refs_0_), channel_id=1, source_target_pairs={{0,6},{2,4},{4,2},{6,0},{8,14},{10,12},{12,10},{14,8},{16,22},{18,... | collective-permute-start | bytes 884744 | tf_op jit(solution)/shard_map/ppermute | solution.py:455
  27.8 19.6 %collective-permute-start.14 = (bf16[4,24,1536]{2,1,0:T(8,128)(2,1)S(1)}, bf16[4,24,1536]{2,1,0:T(8,128)(2,1)S(1)}, u32[]{:S(2)}, u32[]{:S(2)}) collective-permute-start(bf16[4,24,1536]{2,1,0:T(8,128)(2,1)S(1)} %pad_maximum_fusion.refs_0_), channel_id=1, source_target_pairs={{0,4},{2,6},{4,0},{6,2},{8,12},{10,14},{12,8},{14,10},{16,20},{18,... | collective-permute-start | bytes 884744 | tf_op jit(solution)/shard_map/ppermute | solution.py:455
  28.3 19.1 %collective-permute-start.13 = (bf16[4,24,1536]{2,1,0:T(8,128)(2,1)S(1)}, bf16[4,24,1536]{2,1,0:T(8,128)(2,1)S(1)}, u32[]{:S(2)}, u32[]{:S(2)}) collective-permute-start(bf16[4,24,1536]{2,1,0:T(8,128)(2,1)S(1)} %pad_maximum_fusion.refs_0_), channel_id=1, source_target_pairs={{0,2},{2,0},{4,6},{6,4},{8,10},{10,8},{12,14},{14,12},{16,18},{18,... | collective-permute-start | bytes 884744 | tf_op jit(solution)/shard_map/ppermute | solution.py:455
  31.1 15.8 %collective-permute-start.3 = (bf16[4,24,896]{2,1,0:T(8,128)(2,1)S(1)}, bf16[4,24,896]{2,1,0:T(8,128)(2,1)S(1)}, u32[]{:S(2)}, u32[]{:S(2)}) collective-permute-start(bf16[4,24,896]{2,1,0:T(8,128)(2,1)S(1)} %pad_maximum_fusion.1.refs_0_), channel_id=1, source_target_pairs={{0,2},{2,0},{4,6},{6,4},{8,10},{10,8},{12,14},{14,12},{16,18},{18,... | collective-permute-start | bytes 516104 | tf_op jit(solution)/shard_map/ppermute | solution.py:455
  40.5 7.4 %collective-permute-start.9 = (bf16[4,24,896]{2,1,0:T(8,128)(2,1)S(1)}, bf16[4,24,896]{2,1,0:T(8,128)(2,1)S(1)}, u32[]{:S(2)}, u32[]{:S(2)}) collective-permute-start(bf16[4,24,896]{2,1,0:T(8,128)(2,1)S(1)} %collective-permute-done.5.refs_3_), channel_id=1, source_target_pairs={{0,1},{1,0},{2,3},{3,2},{4,5},{5,4},{6,7},{7,6},{8,9},{9,8},{10,11... | collective-permute-start | bytes 516104 | tf_op jit(solution)/shard_map/ppermute | solution.py:459
  46.8 1.4 collective-permute-start.8
  46.9 23.8 %collective-permute-start.16 = (bf16[4,24,1536]{2,1,0:T(8,128)(2,1)S(1)}, bf16[4,24,1536]{2,1,0:T(8,128)(2,1)S(1)}, u32[]{:S(2)}, u32[]{:S(2)}) collective-permute-start(bf16[4,24,1536]{2,1,0:T(8,128)(2,1)S(1)} %pad_maximum_fusion.refs_0_), channel_id=1, source_target_pairs={{0,1},{1,0},{2,3},{3,2},{4,5},{5,4},{6,7},{7,6},{8,9},{9,8},{10,11... | collective-permute-start | bytes 884744 | tf_op jit(solution)/shard_map/ppermute | solution.py:459
  47.4 23.3 %collective-permute-start.19 = (bf16[4,24,1536]{2,1,0:T(8,128)(2,1)S(1)}, bf16[4,24,1536]{2,1,0:T(8,128)(2,1)S(1)}, u32[]{:S(2)}, u32[]{:S(2)}) collective-permute-start(bf16[4,24,1536]{2,1,0:T(8,128)(2,1)S(1)} %collective-permute-done.15.refs_3_), channel_id=1, source_target_pairs={{0,1},{1,0},{2,3},{3,2},{4,5},{5,4},{6,7},{7,6},{8,9},{9,8},{10,11... | collective-permute-start | bytes 884744 | tf_op jit(solution)/shard_map/ppermute | solution.py:459
  47.4 23.3 %collective-permute-start.18 = (bf16[4,24,1536]{2,1,0:T(8,128)(2,1)S(1)}, bf16[4,24,1536]{2,1,0:T(8,128)(2,1)S(1)}, u32[]{:S(2)}, u32[]{:S(2)}) collective-permute-start(bf16[4,24,1536]{2,1,0:T(8,128)(2,1)S(1)} %collective-permute-done.14.refs_2_), channel_id=1, source_target_pairs={{0,1},{1,0},{2,3},{3,2},{4,5},{5,4},{6,7},{7,6},{8,9},{9,8},{10,11... | collective-permute-start | bytes 884744 | tf_op jit(solution)/shard_map/ppermute | solution.py:459
  47.9 22.8 %collective-permute-start.17 = (bf16[4,24,1536]{2,1,0:T(8,128)(2,1)S(1)}, bf16[4,24,1536]{2,1,0:T(8,128)(2,1)S(1)}, u32[]{:S(2)}, u32[]{:S(2)}) collective-permute-start(bf16[4,24,1536]{2,1,0:T(8,128)(2,1)S(1)} %collective-permute-done.13.refs_1_), channel_id=1, source_target_pairs={{0,1},{1,0},{2,3},{3,2},{4,5},{5,4},{6,7},{7,6},{8,9},{9,8},{10,11... | collective-permute-start | bytes 884744 | tf_op jit(solution)/shard_map/ppermute | solution.py:459
  48.3 0.7 copy-start.4
  48.9 1.5 collective-permute-start.7
  49.8 4.1 %copy-start = (bf16[16,197,384]{2,0,1:T(8,128)(2,1)S(1)}, bf16[16,197,384]{2,0,1:T(8,128)(2,1)}, u32[]{:S(2)}) copy-start(bf16[16,197,384]{2,0,1:T(8,128)(2,1)} %param.15) | copy-start | bytes 7262212
  50.5 1.0 copy-start.5
  68.8 1.8 %copy-start.1 = (bf16[8,208,1152]{2,1,0:T(8,128)(2,1)}, bf16[8,208,1152]{2,1,0:T(8,128)(2,1)S(1)}, u32[]{:S(2)}) copy-start(bf16[8,208,1152]{2,1,0:T(8,128)(2,1)S(1)} %get-tuple-element.76.qkv) | copy-start | bytes 11501572
  70.7 1.7 %copy-start.3 = (bf16[16,197,384]{2,0,1:T(8,128)(2,1)S(1)}, bf16[16,197,384]{2,0,1:T(8,128)(2,1)}, u32[]{:S(2)}) copy-start(bf16[16,197,384]{2,0,1:T(8,128)(2,1)} %param.29) | copy-start | bytes 7262212
  95.9 2.9 %collective-permute-start.21 = (bf16[384,1536]{1,0:T(8,128)(2,1)S(1)}, bf16[384,1536]{1,0:T(8,128)(2,1)S(1)}, u32[]{:S(2)}, u32[]{:S(2)}) collective-permute-start(bf16[384,1536]{1,0:T(8,128)(2,1)S(1)} %get-tuple-element.68), channel_id=1, source_target_pairs={{0,1},{1,0},{2,3},{3,2},{4,5},{5,4},{6,7},{7,6},{8,9},{9,8},{10,11... | collective-permute-start | bytes 3538952 | tf_op jit(solution)/shard_map/ppermute | solution.py:459
  96.3 56.6 %collective-permute-start.20 = (bf16[197,8,384]{2,1,0:T(8,128)(2,1)S(1)}, bf16[197,8,384]{2,1,0:T(8,128)(2,1)S(1)}, u32[]{:S(2)}, u32[]{:S(2)}) collective-permute-start(bf16[197,8,384]{2,1,0:T(8,128)(2,1)S(1)} %get-tuple-element.66.own), channel_id=1, source_target_pairs={{0,1},{1,0},{2,3},{3,2},{4,5},{5,4},{6,7},{7,6},{8,9},{9,8},{10,11... | collective-permute-start | bytes 3631112 | tf_op jit(solution)/shard_map/ppermute | solution.py:459
  99.6 2.1 %copy-start.2 = (bf16[8,208,1152]{2,1,0:T(8,128)(2,1)S(1)}, bf16[8,208,1152]{2,1,0:T(8,128)(2,1)}, u32[]{:S(2)}) copy-start(bf16[8,208,1152]{2,1,0:T(8,128)(2,1)} %copy-done.1) | copy-start | bytes 11501572
  125.8 2.6 %collective-permute-start.23 = (bf16[384,896]{1,0:T(8,128)(2,1)S(1)}, bf16[384,896]{1,0:T(8,128)(2,1)S(1)}, u32[]{:S(2)}, u32[]{:S(2)}) collective-permute-start(bf16[384,896]{1,0:T(8,128)(2,1)S(1)} %get-tuple-element.83), channel_id=1, source_target_pairs={{0,1},{1,0},{2,3},{3,2},{4,5},{5,4},{6,7},{7,6},{8,9},{9,8},{10,11... | collective-permute-start | bytes 2064392 | tf_op jit(solution)/shard_map/ppermute | solution.py:459
  126.2 39.2 %collective-permute-start.22 = (bf16[197,8,384]{2,1,0:T(8,128)(2,1)S(1)}, bf16[197,8,384]{2,1,0:T(8,128)(2,1)S(1)}, u32[]{:S(2)}, u32[]{:S(2)}) collective-permute-start(bf16[197,8,384]{2,1,0:T(8,128)(2,1)S(1)} %get-tuple-element.81.own), channel_id=1, source_target_pairs={{0,1},{1,0},{2,3},{3,2},{4,5},{5,4},{6,7},{7,6},{8,9},{9,8},{10,11... | collective-permute-start | bytes 3631112 | tf_op jit(solution)/shard_map/ppermute | solution.py:459
  126.4 9.9 %collective-permute-start.30 = (bf16[4,24,1536]{2,1,0:T(8,128)(2,1)S(1)}, bf16[4,24,1536]{2,1,0:T(8,128)(2,1)S(1)}, u32[]{:S(2)}, u32[]{:S(2)}) collective-permute-start(bf16[4,24,1536]{2,1,0:T(8,128)(2,1)S(1)} %get-tuple-element.101), channel_id=1, source_target_pairs={{0,2},{2,0},{4,6},{6,4},{8,10},{10,8},{12,14},{14,12},{16,18},{18,... | collective-permute-start | bytes 884744 | tf_op jit(solution)/shard_map/ppermute | solution.py:455
  127.9 15.2 %collective-permute-start.31 = (bf16[4,24,1536]{2,1,0:T(8,128)(2,1)S(1)}, bf16[4,24,1536]{2,1,0:T(8,128)(2,1)S(1)}, u32[]{:S(2)}, u32[]{:S(2)}) collective-permute-start(bf16[4,24,1536]{2,1,0:T(8,128)(2,1)S(1)} %get-tuple-element.102), channel_id=1, source_target_pairs={{0,4},{2,6},{4,0},{6,2},{8,12},{10,14},{12,8},{14,10},{16,20},{18,... | collective-permute-start | bytes 884744 | tf_op jit(solution)/shard_map/ppermute | solution.py:455
  128.4 14.8 %collective-permute-start.32 = (bf16[4,24,1536]{2,1,0:T(8,128)(2,1)S(1)}, bf16[4,24,1536]{2,1,0:T(8,128)(2,1)S(1)}, u32[]{:S(2)}, u32[]{:S(2)}) collective-permute-start(bf16[4,24,1536]{2,1,0:T(8,128)(2,1)S(1)} %get-tuple-element.103), channel_id=1, source_target_pairs={{0,6},{2,4},{4,2},{6,0},{8,14},{10,12},{12,10},{14,8},{16,22},{18,... | collective-permute-start | bytes 884744 | tf_op jit(solution)/shard_map/ppermute | solution.py:455
  136.3 9.7 %collective-permute-start.24 = (bf16[4,24,896]{2,1,0:T(8,128)(2,1)S(1)}, bf16[4,24,896]{2,1,0:T(8,128)(2,1)S(1)}, u32[]{:S(2)}, u32[]{:S(2)}) collective-permute-start(bf16[4,24,896]{2,1,0:T(8,128)(2,1)S(1)} %get-tuple-element.85), channel_id=1, source_target_pairs={{0,2},{2,0},{4,6},{6,4},{8,10},{10,8},{12,14},{14,12},{16,18},{18,... | collective-permute-start | bytes 516104 | tf_op jit(solution)/shard_map/ppermute | solution.py:455
  143.1 8.4 %collective-permute-start.25 = (bf16[4,24,896]{2,1,0:T(8,128)(2,1)S(1)}, bf16[4,24,896]{2,1,0:T(8,128)(2,1)S(1)}, u32[]{:S(2)}, u32[]{:S(2)}) collective-permute-start(bf16[4,24,896]{2,1,0:T(8,128)(2,1)S(1)} %get-tuple-element.86), channel_id=1, source_target_pairs={{0,4},{2,6},{4,0},{6,2},{8,12},{10,14},{12,8},{14,10},{16,20},{18,... | collective-permute-start | bytes 516104 | tf_op jit(solution)/shard_map/ppermute | solution.py:455
  143.2 8.4 %collective-permute-start.26 = (bf16[4,24,896]{2,1,0:T(8,128)(2,1)S(1)}, bf16[4,24,896]{2,1,0:T(8,128)(2,1)S(1)}, u32[]{:S(2)}, u32[]{:S(2)}) collective-permute-start(bf16[4,24,896]{2,1,0:T(8,128)(2,1)S(1)} %get-tuple-element.87), channel_id=1, source_target_pairs={{0,6},{2,4},{4,2},{6,0},{8,14},{10,12},{12,10},{14,8},{16,22},{18,... | collective-permute-start | bytes 516104 | tf_op jit(solution)/shard_map/ppermute | solution.py:455
  145.9 9.8 %collective-permute-start.33 = (bf16[1,24,1536]{2,1,0:T(8,128)(2,1)S(1)}, bf16[1,24,1536]{2,1,0:T(8,128)(2,1)S(1)}, u32[]{:S(2)}, u32[]{:S(2)}) collective-permute-start(bf16[1,24,1536]{2,1,0:T(8,128)(2,1)S(1)} %get-tuple-element.105), channel_id=1, source_target_pairs={{0,8},{2,10},{4,12},{6,14},{8,0},{10,2},{12,4},{14,6},{16,24},{18,... | collective-permute-start | bytes 221192 | tf_op jit(solution)/shard_map/ppermute | solution.py:455
  151.5 7.3 %collective-permute-start.34 = (bf16[1,24,1536]{2,1,0:T(8,128)(2,1)S(1)}, bf16[1,24,1536]{2,1,0:T(8,128)(2,1)S(1)}, u32[]{:S(2)}, u32[]{:S(2)}) collective-permute-start(bf16[1,24,1536]{2,1,0:T(8,128)(2,1)S(1)} %get-tuple-element.106), channel_id=1, source_target_pairs={{0,16},{2,18},{4,20},{6,22},{8,24},{10,26},{12,28},{14,30},{16,0},... | collective-permute-start | bytes 221192 | tf_op jit(solution)/shard_map/ppermute | solution.py:455
  151.5 11.4 %collective-permute-start.35 = (bf16[1,24,1536]{2,1,0:T(8,128)(2,1)S(1)}, bf16[1,24,1536]{2,1,0:T(8,128)(2,1)S(1)}, u32[]{:S(2)}, u32[]{:S(2)}) collective-permute-start(bf16[1,24,1536]{2,1,0:T(8,128)(2,1)S(1)} %get-tuple-element.107), channel_id=1, source_target_pairs={{0,24},{2,26},{4,28},{6,30},{8,16},{10,18},{12,20},{14,22},{16,8},... | collective-permute-start | bytes 221192 | tf_op jit(solution)/shard_map/ppermute | solution.py:455
  152.9 10.7 %collective-permute-start.27 = (bf16[1,24,896]{2,1,0:T(8,128)(2,1)S(1)}, bf16[1,24,896]{2,1,0:T(8,128)(2,1)S(1)}, u32[]{:S(2)}, u32[]{:S(2)}) collective-permute-start(bf16[1,24,896]{2,1,0:T(8,128)(2,1)S(1)} %get-tuple-element.89), channel_id=1, source_target_pairs={{0,8},{2,10},{4,12},{6,14},{8,0},{10,2},{12,4},{14,6},{16,24},{18,... | collective-permute-start | bytes 129032 | tf_op jit(solution)/shard_map/ppermute | solution.py:455
  155.7 7.8 %collective-permute-start.28 = (bf16[1,24,896]{2,1,0:T(8,128)(2,1)S(1)}, bf16[1,24,896]{2,1,0:T(8,128)(2,1)S(1)}, u32[]{:S(2)}, u32[]{:S(2)}) collective-permute-start(bf16[1,24,896]{2,1,0:T(8,128)(2,1)S(1)} %get-tuple-element.90), channel_id=1, source_target_pairs={{0,16},{2,18},{4,20},{6,22},{8,24},{10,26},{12,28},{14,30},{16,0},... | collective-permute-start | bytes 129032 | tf_op jit(solution)/shard_map/ppermute | solution.py:455
  158.8 5.8 %collective-permute-start.29 = (bf16[1,24,896]{2,1,0:T(8,128)(2,1)S(1)}, bf16[1,24,896]{2,1,0:T(8,128)(2,1)S(1)}, u32[]{:S(2)}, u32[]{:S(2)}) collective-permute-start(bf16[1,24,896]{2,1,0:T(8,128)(2,1)S(1)} %get-tuple-element.91), channel_id=1, source_target_pairs={{0,24},{2,26},{4,28},{6,30},{8,16},{10,18},{12,20},{14,22},{16,8},... | collective-permute-start | bytes 129032 | tf_op jit(solution)/shard_map/ppermute | solution.py:455
